TPU v7x, 32 devices: a whole 2x2x4 slice. The times are simulated.
32 devices in a mesh: grp: 2 (over x), date: 16 (over z, y, core).
Axes of the slice: x: 2, y: 2, z: 4, core: 2. Of those that a mesh axis runs over, the one named last changes fastest.
Arguments:
- radar_stack: bfloat16 [2, 128, 256, 256], P(None, 'date', 'grp'), parts along dimension 2, may hold values from -6 to 6
- filter_taps: float32 [2, 128, 128], P(None, 'date'), may hold values from -0.6 to 0.6
- filter_lengths: int32 [128], P('date'), may hold values from 64 to 128
- resample_kernel: float32 [4], replicated, may hold values from 0.2 to 1
- tile_owner: int32 [512, 1], P(('grp', 'date')), parts along dimension 0, may hold values from 0 to 15; in each aligned block of 16 rows (0 to 15, 16 to 31, ...) at most 2 rows name the same one
- map_slot: int32 [512], P(('grp', 'date')), parts along dimension 0, may hold values from 0 to 7
- correlation: int32 [512], P(('grp', 'date')), parts along dimension 0, may hold values from 1 to 128
- offsets: int32 [512], P(('grp', 'date')), parts along dimension 0, may hold values from 0 to 127
Outputs:
- geocoded: float32 [256, 256, 128], P(('grp', 'date')), parts along dimension 0
There are 2 independent parts, one for each index of `grp`. A program takes and returns all parts, laid end to end along the dimension named above; an argument that names none is the same for every part. Nothing has to cross between parts.
Inputs may be any that keep to these rules, and one draw needn't show every extreme that they name: `tile_owner`: among the 16 tiles of one device, at most 2 name the same owner.
All inputs are finite; a program needn't handle non-finite values. Where the computation divides by a largest or mean magnitude, that divisor is 1e-20 or more.
Results may differ from a plain program's by a relative error of at most 0.0055.
Values may be sent and summed in bfloat16 or wider, within the bound.
A program may use at most 64 MiB of HBM per device.

v0:
```python
from functools import partial

import jax
import jax.numpy as jnp
from jax import lax
from jax.experimental import pallas as pl
from jax.experimental.pallas import tpu as pltpu
from jax.sharding import PartitionSpec as P

PATCH_AZ = 8
PATCH_RG = 16
TILE = 128
KW = 4
CAP = 2
MAP_DEV = 8
LANES = 128
PHASES = 2
TOGETHER = 4
SWEEPS = 3

diag_load = 0.5
small_eps = 1e-05
MESH = pl.DeviceIdType.MESH
VMEM = pl.BlockSpec(memory_space=pltpu.VMEM)
HBM = pl.BlockSpec(memory_space=pltpu.MemorySpace.HBM)
BIG = 32 * 1024 * 1024


def whiten_window(zt):
    looks, dates = zt.shape[0], zt.shape[1] // 2
    gram = lax.dot_general(zt, zt, (((0,), (0,)), ((), ())), preferred_element_type=jnp.float32)
    gram_re = (gram[:dates, :dates] + gram[dates:, dates:]) * (1.0 / looks)
    gram_im = (gram[dates:, :dates] - gram[:dates, dates:]) * (1.0 / looks)
    eye = lax.broadcasted_iota(jnp.int32, (dates, dates), 0) == lax.broadcasted_iota(
        jnp.int32, (dates, dates), 1
    )
    diagonal = jnp.where(eye, gram_re, 0.0)
    scale_col = lax.rsqrt(jnp.sum(diagonal, axis=1, keepdims=True) + small_eps)
    scale_row = lax.rsqrt(jnp.sum(diagonal, axis=0, keepdims=True) + small_eps)
    outer = scale_col * scale_row
    coher_re = gram_re * outer + jnp.where(eye, diag_load, 0.0)
    coher_im = gram_im * outer
    sums = jnp.sum(jnp.abs(coher_re) + jnp.abs(coher_im), axis=1, keepdims=True)
    over = 1.0 / jnp.max(sums, axis=0, keepdims=True)

    part_re, part_im = coher_re * over, coher_im * over
    w, rounded = zt.astype(jnp.float32), zt
    for stage in range(SWEEPS):
        re, im = part_re.astype(jnp.bfloat16), part_im.astype(jnp.bfloat16)
        top = jnp.concatenate([re, -im], axis=1)
        whole = jnp.concatenate([top, jnp.concatenate([im, re], axis=1)], axis=0)
        if stage < SWEEPS - 1:
            both = jnp.dot(jnp.concatenate([top, rounded], axis=0), whole, preferred_element_type=jnp.float32)
            part_re = 2.0 * part_re - both[:dates, :dates]
            part_im = 2.0 * part_im + both[:dates, dates:]
            applied = both[dates:]
        else:
            applied = jnp.dot(rounded, whole, preferred_element_type=jnp.float32)
        w = 2.0 * w - applied
        rounded = w.astype(jnp.bfloat16)
    return (w * over).astype(jnp.bfloat16)


def flow_kernel(n, *refs):
    inputs, refs = refs[:9], refs[9:]
    result_ref, cells_ref, got_cells, facts_ref, got_facts, cell_ref, z_ref, tiles_ref, out_msg, got_msg = refs[:10]
    total_ref, den_ref, operator_ref, table_ref = refs[10:14]
    local, refs = refs[14:23], refs[23:]
    len_ref, owner_ref, kern_ref, radar_ref, taps_ref = local[:5]
    fact_refs = local[5:]
    own_sem, fact_send, fact_recv, cell_send, cell_recv, msg_send, msg_recv, load_sem = refs
    me = lax.axis_index("date")
    dates_here, rows = radar_ref.shape[1], radar_ref.shape[2]
    taps, tile_count = taps_ref.shape[2], owner_ref.shape[0]
    total = n * dates_here
    half = LANES // PHASES
    windows = LANES // PATCH_RG

    barrier = pltpu.get_barrier_semaphore()
    loads = [pltpu.make_async_copy(x, y, load_sem.at[i]) for i, (x, y) in enumerate(zip(inputs, local))]
    for load in loads:
        load.start()
    for k in range(1, n):
        pl.semaphore_signal(barrier, inc=1, device_id={"date": lax.rem(me + k, n)}, device_id_type=MESH)
    own = [pltpu.make_async_copy(cells_ref.at[h, me], got_cells.at[h, me], own_sem.at[h]) for h in range(PHASES)]
    own.append(pltpu.make_async_copy(facts_ref, got_facts.at[me], own_sem.at[PHASES]))

    def remote(src, dst, send, recv, peer):
        return pltpu.make_async_remote_copy(
            src_ref=src, dst_ref=dst, send_sem=send, recv_sem=recv, device_id={"date": peer}, device_id_type=MESH
        )

    def fact_copy(peer, origin):
        return remote(facts_ref, got_facts.at[origin], fact_send.at[peer], fact_recv.at[origin], peer)

    def cell_copy(h, peer, origin):
        return remote(
            cells_ref.at[h, peer], got_cells.at[h, origin], cell_send.at[h, peer], cell_recv.at[h, origin], peer
        )

    def msg_copy(h, peer, origin):
        return remote(
            out_msg.at[h, peer], got_msg.at[h, origin], msg_send.at[h, peer], msg_recv.at[h, origin], peer
        )

    def partner(k):
        peer, bit = me, 1
        while bit < n:
            peer = peer + (k // bit) % 2 * (1 - (me // bit) % 2 * 2) * bit
            bit *= 2
        return peer

    def turn(i):
        return n - 1 - i // 2 - i % 2 * (n // 2)

    peers = [turn(i) for i in range(n - 1)]

    for load in loads:
        load.wait()
    facts_ref[...] = jnp.full(facts_ref.shape, -1, jnp.int32)
    for i, fact in enumerate(fact_refs):
        facts_ref[pl.ds(i, 1), pl.ds(0, tile_count)] = fact[...]
    position = lax.broadcasted_iota(jnp.int32, (1, taps), 1)
    a_iota = lax.broadcasted_iota(jnp.int32, (rows, rows), 0)
    b_iota = lax.broadcasted_iota(jnp.int32, (rows, rows), 1)
    tap_at = b_iota - a_iota + taps // 2
    inside = jnp.logical_and(tap_at >= 0, tap_at < taps)
    low = lax.broadcasted_iota(jnp.int32, (2 * rows, LANES), 1) < half

    def toeplitz(d, which):
        kept = jnp.where(position < len_ref[d], taps_ref[which, pl.ds(d, 1), :], 0.0)
        rolled = pltpu.roll(jnp.broadcast_to(kept, (rows, taps)), taps // 2, 1, stride=1, stride_axis=0)
        return jnp.where(inside, jnp.concatenate([rolled] * (rows // taps), axis=1), 0.0)

    for h in range(PHASES):
        for d in range(dates_here):
            if h == 0:
                t_re, t_im = toeplitz(d, 0), toeplitz(d, 1)
                operator_ref[d] = jnp.concatenate(
                    [jnp.concatenate([t_re, -t_im], axis=1), jnp.concatenate([t_im, t_re], axis=1)], axis=0
                ).astype(jnp.bfloat16)
            columns = jnp.concatenate([radar_ref[0, d], radar_ref[1, d]], axis=0).astype(jnp.float32)
            sides = [columns[:, c * LANES : (c + 1) * LANES] for c in range(2)]
            sides[1 - h] = pltpu.roll(sides[1 - h], half, 1)
            product = jnp.dot(
                operator_ref[d],
                jnp.where(low, sides[0], sides[1]).astype(jnp.bfloat16),
                preferred_element_type=jnp.float32,
            )
            for p in range(n):
                for part in range(2):
                    top = part * rows + p * PATCH_AZ
                    cell_ref[p, pl.ds(part * PATCH_AZ * dates_here + d, PATCH_AZ, stride=dates_here), :] = product[
                        top : top + PATCH_AZ
                    ]
        for p in range(n):
            cells_ref[h, p] = cell_ref[p].astype(jnp.bfloat16)
        if h == 0:
            pl.semaphore_wait(barrier, n - 1)
        for k in peers:
            cell_copy(h, partner(k), me).start()
        own[h].start()
        if h == 0:
            for k in peers:
                fact_copy(partner(k), me).start()
            own[PHASES].start()

    owners = [owner_ref[t] for t in range(tile_count)]
    for o in range(n):
        first, last = 0, 0
        for t in range(tile_count):
            last = jnp.where(owners[t] == o, t, last)
            first = jnp.where(owners[tile_count - 1 - t] == o, tile_count - 1 - t, first)
        table_ref[o * CAP] = first
        table_ref[o * CAP + 1] = last

    per_half = windows // 2
    for h in range(PHASES):
        own[h].wait()
        for k in peers:
            cell_copy(h, partner(k), partner(k)).wait_recv()
        for s in range(n):
            cell_ref[s] = got_cells[h, s].astype(jnp.float32)
        for part in range(2):
            for a in range(PATCH_AZ):
                at = pl.ds((part * PATCH_AZ + a) * dates_here, dates_here)
                line = jnp.concatenate([cell_ref[s, at, :] for s in range(n)], axis=0).T.astype(jnp.bfloat16)
                for j in range(windows):
                    z_ref[j, a * PATCH_RG : (a + 1) * PATCH_RG, part * total : (part + 1) * total] = line[
                        j * PATCH_RG : (j + 1) * PATCH_RG
                    ]

        def whiten(i, carry):
            for q in range(TOGETHER):
                side = i * TOGETHER // per_half
                j = i * TOGETHER % per_half + q
                white = whiten_window(z_ref[i * TOGETHER + q])
                for a in range(PATCH_AZ):
                    tiles_ref[a * 2 + side, pl.ds(j * PATCH_RG, PATCH_RG), :] = white[
                        a * PATCH_RG : (a + 1) * PATCH_RG
                    ]
            return carry

        lax.fori_loop(0, windows // TOGETHER, whiten, 0)

        def message(o, i):
            return tiles_ref[table_ref[o * CAP + i]]

        def pack(k, carry):
            o = partner(k)
            for i in range(CAP):
                out_msg[h, o, pl.ds(i * half, half), :] = message(o, i)
            return carry

        lax.fori_loop(1, n, pack, 0)
        for i in range(CAP):
            got_msg[h, me, pl.ds(i * half, half), :] = message(me, i)
        for k in peers:
            msg_copy(h, partner(k), me).start()

    total_ref[...] = jnp.zeros(total_ref.shape, jnp.float32)
    den_ref[...] = jnp.zeros(den_ref.shape, jnp.float32)
    apart = lax.broadcasted_iota(jnp.int32, (TILE, TILE), 1) - lax.broadcasted_iota(jnp.int32, (TILE, TILE), 0) + TILE
    lane = lax.broadcasted_iota(jnp.int32, (1, LANES), 1)
    map_row = lax.broadcasted_iota(jnp.int32, den_ref.shape, 0)

    def gather(s):
        facts = got_facts[s].astype(jnp.float32)
        mine = got_facts[s, pl.ds(0, 1), :] == me
        place = lane.astype(jnp.float32)
        first = jnp.min(jnp.where(mine, place, 2.0 * LANES), axis=1, keepdims=True)
        last = jnp.max(jnp.where(mine, place, -1.0), axis=1, keepdims=True)
        moved, weights = [], []
        for i, at in enumerate((first, last)):
            picked = jnp.sum(jnp.where(place == at, facts, 0.0), axis=1, keepdims=True)
            slot, shift, corr = picked[1:2], picked[2:3].astype(jnp.int32), picked[3:4]
            if i:
                corr = jnp.where(last > first, corr, 0.0)
            step = (apart - shift) & (TILE - 1)
            circ = jnp.zeros((TILE, TILE), jnp.float32)
            for k in range(KW):
                circ = jnp.where(step == k, kern_ref[k], circ)
            x = jnp.concatenate([got_msg[h, s, pl.ds(i * half, half), :] for h in range(PHASES)], axis=0)
            moved.append(jnp.dot(circ.astype(jnp.bfloat16), x, preferred_element_type=jnp.float32))
            weights.append(jnp.where(map_row == slot.astype(jnp.int32), corr, 0.0))
        den_ref[...] += weights[0] + weights[1]
        for m in range(MAP_DEV):
            total_ref[m] += weights[0][m : m + 1, :1] * moved[0] + weights[1][m : m + 1, :1] * moved[1]

    own[PHASES].wait()
    gather(me)

    def arrive(i, carry):
        s = partner(turn(i))
        fact_copy(s, s).wait_recv()
        for h in range(PHASES):
            msg_copy(h, s, s).wait_recv()
        gather(s)
        return carry

    lax.fori_loop(0, n - 1, arrive, 0)
    for m in range(MAP_DEV):
        result_ref[m] = (total_ref[m] / jnp.maximum(den_ref[m : m + 1, :1], 1.0)).T
    for k in peers:
        fact_copy(partner(k), me).wait_send()
        for h in range(PHASES):
            cell_copy(h, partner(k), me).wait_send()
            msg_copy(h, partner(k), me).wait_send()


def shards(n, radar_stack, filter_taps, filter_lengths, resample_kernel, tile_owner, map_slot, correlation, offsets):
    dates_here, rows, ranges = radar_stack.shape[1:]
    dates = n * dates_here
    tile_count = tile_owner.shape[0]
    block = (PHASES, n, 2 * PATCH_AZ * dates_here, LANES)
    message = (PHASES, n, LANES, 2 * dates)
    facts = [x.reshape(1, tile_count) for x in (tile_owner, map_slot, offsets, correlation)]

    dma = pltpu.SemaphoreType.DMA
    return pl.pallas_call(
        partial(flow_kernel, n),
        out_shape=jax.ShapeDtypeStruct((MAP_DEV, 2 * dates, TILE), jnp.float32),
        in_specs=[HBM] * 9,
        out_specs=VMEM,
        scratch_shapes=[
            pltpu.VMEM(block, jnp.bfloat16),
            pltpu.VMEM(block, jnp.bfloat16),
            pltpu.VMEM((8, LANES), jnp.int32),
            pltpu.VMEM((n, 8, LANES), jnp.int32),
            pltpu.VMEM(block[1:], jnp.float32),
            pltpu.VMEM((LANES // PATCH_RG, LANES, 2 * dates), jnp.bfloat16),
            pltpu.VMEM((tile_count, LANES // PHASES, 2 * dates), jnp.bfloat16),
            pltpu.VMEM(message, jnp.bfloat16),
            pltpu.VMEM(message, jnp.bfloat16),
            pltpu.VMEM((MAP_DEV, TILE, 2 * dates), jnp.float32),
            pltpu.VMEM((MAP_DEV, TILE), jnp.float32),
            pltpu.VMEM((dates_here, 2 * rows, 2 * rows), jnp.bfloat16),
            pltpu.SMEM((n * CAP,), jnp.int32),
            pltpu.SMEM(filter_lengths.shape, jnp.int32),
            pltpu.SMEM((tile_count,), jnp.int32),
            pltpu.SMEM(resample_kernel.shape, jnp.float32),
            pltpu.VMEM(radar_stack.shape, radar_stack.dtype),
            pltpu.VMEM(filter_taps.shape, jnp.float32),
            pltpu.VMEM((1, tile_count), jnp.int32),
            pltpu.VMEM((1, tile_count), jnp.int32),
            pltpu.VMEM((1, tile_count), jnp.int32),
            pltpu.VMEM((1, tile_count), jnp.int32),
            dma((PHASES + 1,)),
            dma((n,)),
            dma((n,)),
            dma((PHASES, n)),
            dma((PHASES, n)),
            dma((PHASES, n)),
            dma((PHASES, n)),
            dma((9,)),
        ],
        compiler_params=pltpu.CompilerParams(collective_id=0, has_side_effects=True, vmem_limit_bytes=BIG),
        name="flow",
    )(*[pltpu.with_memory_space_constraint(x, pltpu.MemorySpace.HBM) for x in (filter_lengths, tile_owner.reshape(tile_count), resample_kernel, radar_stack, filter_taps, *facts)])


def solution(mesh):
    in_specs = (
        P(None, "date", "grp", None),
        P(None, "date", None),
        P("date"),
        P(),
        P(("grp", "date"), None),
        P(("grp", "date")),
        P(("grp", "date")),
        P(("grp", "date")),
    )
    out_specs = P(("grp", "date"), None, None)
    return jax.shard_map(
        partial(shards, mesh.shape["date"]), mesh=mesh, in_specs=in_specs, out_specs=out_specs, check_vma=False
    )
```

profile of v0, /device:TPU:0, one launch (start us, length us, event | category | flops | bytes accessed | tf_op | source)
XLA Modules:
  0.0 80.1 jit_solution(6635232067667068726)
XLA Ops:
  0.0 79.1 %flow.1 = f32[8,256,128]{2,1,0:T(8,128)S(1)} custom-call(s32[8]{0:T(128)} %refs_0_.1, s32[16]{0:T(128)} %bitcast.5, f32[4]{0:T(128)} %refs_2_.1, bf16[2,8,128,256]{3,2,1,0:T(8,128)(2,1)} %refs_3_.1, f32[2,8,128]{2,1,0:T(8,128)} %refs_4_.1, s32[1,16]{1,0:T(1,128)} %bitcast.6, s32[1,16]{1,0:T(1,128)} %bitcast.7, s32[1,16]{1,0:T(1,128)} %bitcast.8, s32[1,16]{1,0:T(1,128)} %bitcast.9), custom_call_target="tpu_custom_call" | custom-call | tf_op jit(solution)/shard_map/flow/pallas_call | solution.py:280
  79.1 1.0 %copy.10 = f32[8,256,128]{2,1,0:T(8,128)} copy(f32[8,256,128]{2,1,0:T(8,128)S(1)} %flow.1) | data formatting | bytes 2097152
where the time goes:
time: 80.2 us; the launch traced here: 80.1 us
  Pallas kernels  79.1 us (99%)
  local copies, waits for them, and re-layouts  0.97 us (1%)
    pallas_call x1, Pallas kernels, shards(): pl.pallas_call(partial(flow_kernel, n), out_shape=jax.ShapeDtypeStruct((M...  79.1 us

commit v1 on v0

v1 whole, which is shorter than its diff:
```python
from functools import partial

import jax
import jax.numpy as jnp
from jax import lax
from jax.experimental import pallas as pl
from jax.experimental.pallas import tpu as pltpu
from jax.sharding import PartitionSpec as P

PATCH_AZ = 8
PATCH_RG = 16
TILE = 128
KW = 4
MAP_DEV = 8
LANES = 128
PHASES = 2
TOGETHER = 4
GROUPS = 2
CHUNKS = 4
FACTS = 8
SWEEPS = 3

diag_load = 0.5
small_eps = 1e-05
MESH = pl.DeviceIdType.MESH
VMEM = pl.BlockSpec(memory_space=pltpu.VMEM)
HBM = pl.BlockSpec(memory_space=pltpu.MemorySpace.HBM)
BIG = 32 * 1024 * 1024


def whiten_window(zt):
    looks, dates = zt.shape[0], zt.shape[1] // 2
    gram = lax.dot_general(zt, zt, (((0,), (0,)), ((), ())), preferred_element_type=jnp.float32)
    gram_re = (gram[:dates, :dates] + gram[dates:, dates:]) * (1.0 / looks)
    gram_im = (gram[dates:, :dates] - gram[:dates, dates:]) * (1.0 / looks)
    eye = lax.broadcasted_iota(jnp.int32, (dates, dates), 0) == lax.broadcasted_iota(
        jnp.int32, (dates, dates), 1
    )
    diagonal = jnp.where(eye, gram_re, 0.0)
    scale_col = lax.rsqrt(jnp.sum(diagonal, axis=1, keepdims=True) + small_eps)
    scale_row = lax.rsqrt(jnp.sum(diagonal, axis=0, keepdims=True) + small_eps)
    outer = scale_col * scale_row
    coher_re = gram_re * outer + jnp.where(eye, diag_load, 0.0)
    coher_im = gram_im * outer
    sums = jnp.sum(jnp.abs(coher_re) + jnp.abs(coher_im), axis=1, keepdims=True)
    over = 1.0 / jnp.max(sums, axis=0, keepdims=True)

    part_re, part_im = coher_re * over, coher_im * over
    w, rounded = zt.astype(jnp.float32), zt
    for stage in range(SWEEPS):
        re, im = part_re.astype(jnp.bfloat16), part_im.astype(jnp.bfloat16)
        top = jnp.concatenate([re, -im], axis=1)
        whole = jnp.concatenate([top, jnp.concatenate([im, re], axis=1)], axis=0)
        if stage < SWEEPS - 1:
            both = jnp.dot(jnp.concatenate([top, rounded], axis=0), whole, preferred_element_type=jnp.float32)
            part_re = 2.0 * part_re - both[:dates, :dates]
            part_im = 2.0 * part_im + both[:dates, dates:]
            applied = both[dates:]
        else:
            applied = jnp.dot(rounded, whole, preferred_element_type=jnp.float32)
        w = 2.0 * w - applied
        rounded = w.astype(jnp.bfloat16)
    return (w * over).astype(jnp.bfloat16)


def flow_kernel(n, *refs):
    inputs, refs = refs[:8], refs[8:]
    result_ref, cells_ref, got_cells, facts_ref, got_facts, cell_ref, z_ref, white_ref, flat_ref = refs[:9]
    row_msg, got_rows, sums_ref, sum_msg, got_sums, operator_ref, spread_ref, bits_ref, inv_ref = refs[9:18]
    local, refs = refs[18:26], refs[26:]
    len_ref, kern_ref, radar_ref, taps_ref = local[:4]
    fact_refs = local[4:8]
    own_sem, fact_send, fact_recv, cell_send, cell_recv, row_send, row_recv, sum_send, sum_recv, load_sem = refs
    me = lax.axis_index("date")
    dates_here, rows = radar_ref.shape[1], radar_ref.shape[2]
    taps, tile_count = taps_ref.shape[2], fact_refs[0].shape[1]
    total = n * dates_here
    half = LANES // PHASES
    windows = LANES // PATCH_RG
    near = n // GROUPS
    group, rank = me // near, me % near
    tiles = near * tile_count
    deep = 2 * total // near // CHUNKS

    barrier = pltpu.get_barrier_semaphore()
    loads = [pltpu.make_async_copy(x, y, load_sem.at[i]) for i, (x, y) in enumerate(zip(inputs, local))]
    for load in loads:
        load.start()
    for k in range(1, n):
        pl.semaphore_signal(barrier, inc=1, device_id={"date": lax.rem(me + k, n)}, device_id_type=MESH)
    own = [pltpu.make_async_copy(cells_ref.at[h, me], got_cells.at[h, me], own_sem.at[h]) for h in range(PHASES)]

    def remote(src, dst, send, recv, peer):
        return pltpu.make_async_remote_copy(
            src_ref=src, dst_ref=dst, send_sem=send, recv_sem=recv, device_id={"date": peer}, device_id_type=MESH
        )

    def fact_copy(peer, origin):
        return remote(facts_ref, got_facts.at[origin], fact_send.at[peer], fact_recv.at[origin], peer)

    def cell_copy(h, peer, origin):
        return remote(
            cells_ref.at[h, peer], got_cells.at[h, origin], cell_send.at[h, peer], cell_recv.at[h, origin], peer
        )

    def row_copy(h, q, peer, origin):
        to, come = peer % near, origin % near
        return remote(
            row_msg.at[h, to, q], got_rows.at[h, come, q], row_send.at[h, q, to], row_recv.at[h, q, come], peer
        )

    def sum_copy(q, peer, origin):
        return remote(
            sum_msg.at[q, peer], got_sums.at[q, origin], sum_send.at[q, peer], sum_recv.at[q, origin], peer
        )

    def partner(k):
        peer, bit = me, 1
        while bit < n:
            peer = peer + (k // bit) % 2 * (1 - (me // bit) % 2 * 2) * bit
            bit *= 2
        return peer

    def turn(i):
        return n - 1 - i // 2 - i % 2 * (n // 2)

    peers = [turn(i) for i in range(n - 1)]
    inner = list(range(near - 1, 0, -1))

    for load in loads:
        load.wait()
    position = lax.broadcasted_iota(jnp.int32, (1, taps), 1)
    a_iota = lax.broadcasted_iota(jnp.int32, (rows, rows), 0)
    b_iota = lax.broadcasted_iota(jnp.int32, (rows, rows), 1)
    tap_at = b_iota - a_iota + taps // 2
    inside = jnp.logical_and(tap_at >= 0, tap_at < taps)
    low = lax.broadcasted_iota(jnp.int32, (2 * rows, LANES), 1) < half

    def toeplitz(d, which):
        kept = jnp.where(position < len_ref[d], taps_ref[which, pl.ds(d, 1), :], 0.0)
        rolled = pltpu.roll(jnp.broadcast_to(kept, (rows, taps)), taps // 2, 1, stride=1, stride_axis=0)
        return jnp.where(inside, jnp.concatenate([rolled] * (rows // taps), axis=1), 0.0)

    for h in range(PHASES):
        for d in range(dates_here):
            if h == 0:
                t_re, t_im = toeplitz(d, 0), toeplitz(d, 1)
                operator_ref[d] = jnp.concatenate(
                    [jnp.concatenate([t_re, -t_im], axis=1), jnp.concatenate([t_im, t_re], axis=1)], axis=0
                ).astype(jnp.bfloat16)
            columns = jnp.concatenate([radar_ref[0, d], radar_ref[1, d]], axis=0).astype(jnp.float32)
            sides = [columns[:, c * LANES : (c + 1) * LANES] for c in range(2)]
            sides[1 - h] = pltpu.roll(sides[1 - h], half, 1)
            product = jnp.dot(
                operator_ref[d],
                jnp.where(low, sides[0], sides[1]).astype(jnp.bfloat16),
                preferred_element_type=jnp.float32,
            )
            for p in range(n):
                for part in range(2):
                    top = part * rows + p * PATCH_AZ
                    cell_ref[p, pl.ds(part * PATCH_AZ * dates_here + d, PATCH_AZ, stride=dates_here), :] = product[
                        top : top + PATCH_AZ
                    ]
        for p in range(n):
            cells_ref[h, p] = cell_ref[p].astype(jnp.bfloat16)
        if h == 0:
            pl.semaphore_wait(barrier, n - 1)
        for k in peers:
            cell_copy(h, partner(k), me).start()
        own[h].start()

    tile_at = lax.broadcasted_iota(jnp.int32, (LANES, tiles), 0)
    lane_at = lax.broadcasted_iota(jnp.int32, (LANES, tiles), 1)
    placed = (tile_at & 1) * (tiles // 2) + rank * PATCH_AZ + (tile_at >> 1)
    moving = jnp.where(jnp.logical_and(lane_at == placed, tile_at < tile_count), 1.0, 0.0).astype(jnp.bfloat16)
    listed = jnp.concatenate([fact[...] for fact in fact_refs], axis=0).astype(jnp.float32)
    listed = jnp.concatenate([listed, jnp.zeros((FACTS - 4, tile_count), jnp.float32)], axis=0)
    listed = jnp.concatenate([listed, jnp.zeros((FACTS, LANES - tile_count), jnp.float32)], axis=1)
    facts_ref[...] = jnp.dot(listed.astype(jnp.bfloat16), moving, preferred_element_type=jnp.float32)
    for k in peers:
        fact_copy(partner(k), me).start()
    got_facts[me] = facts_ref[...]
    for k in peers:
        fact_copy(partner(k), partner(k)).wait_recv()

    here = got_facts[group * near]
    for s in range(1, near):
        here = here + got_facts[group * near + s]
    target = here[0:1] * MAP_DEV + here[1:2]
    map_at = lax.broadcasted_iota(jnp.int32, (n * MAP_DEV, tiles), 0).astype(jnp.float32)
    spread_ref[...] = jnp.where(map_at == target, here[3:4], 0.0).astype(jnp.bfloat16)
    for j in range(tiles // LANES):
        shift = jnp.broadcast_to(here[2:3, j * LANES : (j + 1) * LANES], (LANES, LANES)).T.astype(jnp.int32)
        for b in range(bits_ref.shape[0]):
            bits_ref[b, j * LANES : (j + 1) * LANES] = (shift >> b) & 1
    mine = me * MAP_DEV + lax.broadcasted_iota(jnp.int32, (MAP_DEV, tiles), 0)
    count = jnp.zeros((MAP_DEV, tiles), jnp.float32)
    for k in range(GROUPS):
        facts = got_facts[k * near]
        for s in range(1, near):
            facts = facts + got_facts[k * near + s]
        count = count + jnp.where(mine.astype(jnp.float32) == facts[0:1] * MAP_DEV + facts[1:2], facts[3:4], 0.0)
    inv_ref[...] = jnp.broadcast_to(
        1.0 / jnp.maximum(jnp.sum(count, axis=1, keepdims=True), 1.0), inv_ref.shape
    )

    per_half = windows // 2
    for h in range(PHASES):
        own[h].wait()
        for k in peers:
            cell_copy(h, partner(k), partner(k)).wait_recv()
        for s in range(n):
            cell_ref[s] = got_cells[h, s].astype(jnp.float32)
        for part in range(2):
            for a in range(PATCH_AZ):
                at = pl.ds((part * PATCH_AZ + a) * dates_here, dates_here)
                line = jnp.concatenate([cell_ref[s, at, :] for s in range(n)], axis=0).T.astype(jnp.bfloat16)
                for j in range(windows):
                    z_ref[j, a * PATCH_RG : (a + 1) * PATCH_RG, part * total : (part + 1) * total] = line[
                        j * PATCH_RG : (j + 1) * PATCH_RG
                    ]

        def whiten(i, carry):
            for q in range(TOGETHER):
                w = i * TOGETHER + q
                white = whiten_window(z_ref[w])
                for a in range(PATCH_AZ):
                    white_ref[a, pl.ds(w * PATCH_RG, PATCH_RG), :] = white[a * PATCH_RG : (a + 1) * PATCH_RG]
            return carry

        lax.fori_loop(0, windows // TOGETHER, whiten, 0)

        for a in range(PATCH_AZ):
            tall = white_ref[a].astype(jnp.float32)
            for part in range(2):
                flat_ref[pl.ds(part * total * PATCH_AZ + a, total, stride=PATCH_AZ), :] = tall[
                    :, part * total : (part + 1) * total
                ].T
        for q in range(CHUNKS):
            for to in range(near):
                row_msg[h, to, q] = flat_ref[
                    pl.ds((to * CHUNKS + q) * deep * PATCH_AZ, deep * PATCH_AZ), :
                ].astype(jnp.bfloat16)
            got_rows[h, rank, q] = row_msg[h, rank, q]
            for k in inner:
                row_copy(h, q, partner(k), me).start()

    first_half = lax.broadcasted_iota(jnp.int32, (tiles // 2, LANES), 1) < half

    def reduce(q, carry):
        for k in inner:
            for h in range(PHASES):
                row_copy(h, q, partner(k), partner(k)).wait_recv()

        def pair(i, carry):
            at = pl.ds(pl.multiple_of(i * 2 * PATCH_AZ, 2 * PATCH_AZ), 2 * PATCH_AZ)
            both = [[got_rows[h, s, q, at, :].astype(jnp.float32) for s in range(near)] for h in range(PHASES)]
            wide = []
            for r in range(2):
                one, two = [
                    jnp.concatenate([x[r * PATCH_AZ : (r + 1) * PATCH_AZ] for x in both[h]], axis=0) for h in range(2)
                ]
                y = jnp.concatenate(
                    [
                        jnp.where(first_half, one, pltpu.roll(two, half, 1)),
                        jnp.where(first_half, pltpu.roll(one, half, 1), two),
                    ],
                    axis=0,
                )
                for b in range(bits_ref.shape[0]):
                    y = jnp.where(bits_ref[b] != 0, pltpu.roll(y, LANES - (1 << b), 1), y)
                wide.append(y.astype(jnp.bfloat16))
            out = jnp.dot(spread_ref[...], jnp.concatenate(wide, axis=1), preferred_element_type=jnp.float32)
            for r in range(2):
                for o in range(n):
                    sums_ref[o, pl.ds(i * 2 + r, MAP_DEV, stride=deep), :] = out[
                        o * MAP_DEV : (o + 1) * MAP_DEV, r * LANES : (r + 1) * LANES
                    ]
            return carry

        lax.fori_loop(0, deep // 2, pair, 0)
        for o in range(n):
            sum_msg[q, o] = sums_ref[o].astype(jnp.bfloat16)
        got_sums[q, me] = sum_msg[q, me]
        for k in peers:
            sum_copy(q, partner(k), me).start()
        return carry

    lax.fori_loop(0, CHUNKS, reduce, 0)

    weights = [kern_ref[k].astype(jnp.bfloat16).astype(jnp.float32) for k in range(KW)]

    def finish(q, carry):
        for k in peers:
            sum_copy(q, partner(k), partner(k)).wait_recv()

        def place(s, carry):
            y = got_sums[q, s].astype(jnp.float32)
            for k in range(1, GROUPS):
                y = y + got_sums[q, s + k * near].astype(jnp.float32)
            out = weights[0] * y
            for k in range(1, KW):
                out = out + weights[k] * pltpu.roll(y, LANES - k, 1)
            at = pl.ds(pl.multiple_of((s * CHUNKS + q) * deep, deep), deep)
            for m in range(MAP_DEV):
                result_ref[m, at, :] = out[m * deep : (m + 1) * deep] * inv_ref[m : m + 1, :]
            return carry

        lax.fori_loop(0, near, place, 0)
        return carry

    lax.fori_loop(0, CHUNKS, finish, 0)

    for k in peers:
        fact_copy(partner(k), me).wait_send()
        for h in range(PHASES):
            cell_copy(h, partner(k), me).wait_send()
        for q in range(CHUNKS):
            sum_copy(q, partner(k), me).wait_send()
    for k in inner:
        for h in range(PHASES):
            for q in range(CHUNKS):
                row_copy(h, q, partner(k), me).wait_send()


def shards(n, radar_stack, filter_taps, filter_lengths, resample_kernel, tile_owner, map_slot, correlation, offsets):
    dates_here, rows, ranges = radar_stack.shape[1:]
    dates = n * dates_here
    tile_count = tile_owner.shape[0]
    near = n // GROUPS
    tiles = near * tile_count
    deep = 2 * dates // near // CHUNKS
    block = (PHASES, n, 2 * PATCH_AZ * dates_here, LANES)
    row_block = (PHASES, near, CHUNKS, deep * PATCH_AZ, LANES)
    sum_block = (CHUNKS, n, MAP_DEV * deep, LANES)
    facts = [x.reshape(1, tile_count) for x in (tile_owner, map_slot, offsets, correlation)]
    given = (filter_lengths, resample_kernel, radar_stack, filter_taps, *facts)

    dma = pltpu.SemaphoreType.DMA
    return pl.pallas_call(
        partial(flow_kernel, n),
        out_shape=jax.ShapeDtypeStruct((MAP_DEV, 2 * dates, TILE), jnp.float32),
        in_specs=[HBM] * len(given),
        out_specs=VMEM,
        scratch_shapes=[
            pltpu.VMEM(block, jnp.bfloat16),
            pltpu.VMEM(block, jnp.bfloat16),
            pltpu.VMEM((FACTS, tiles), jnp.float32),
            pltpu.VMEM((n, FACTS, tiles), jnp.float32),
            pltpu.VMEM(block[1:], jnp.float32),
            pltpu.VMEM((LANES // PATCH_RG, LANES, 2 * dates), jnp.bfloat16),
            pltpu.VMEM((PATCH_AZ, LANES, 2 * dates), jnp.bfloat16),
            pltpu.VMEM((2 * dates * PATCH_AZ, LANES), jnp.float32),
            pltpu.VMEM(row_block, jnp.bfloat16),
            pltpu.VMEM(row_block, jnp.bfloat16),
            pltpu.VMEM(sum_block[1:], jnp.float32),
            pltpu.VMEM(sum_block, jnp.bfloat16),
            pltpu.VMEM(sum_block, jnp.bfloat16),
            pltpu.VMEM((dates_here, 2 * rows, 2 * rows), jnp.bfloat16),
            pltpu.VMEM((n * MAP_DEV, tiles), jnp.bfloat16),
            pltpu.VMEM(((TILE - 1).bit_length(), tiles, LANES), jnp.int32),
            pltpu.VMEM((MAP_DEV, LANES), jnp.float32),
            pltpu.SMEM(filter_lengths.shape, jnp.int32),
            pltpu.SMEM(resample_kernel.shape, jnp.float32),
            pltpu.VMEM(radar_stack.shape, radar_stack.dtype),
            pltpu.VMEM(filter_taps.shape, jnp.float32),
            pltpu.VMEM((1, tile_count), jnp.int32),
            pltpu.VMEM((1, tile_count), jnp.int32),
            pltpu.VMEM((1, tile_count), jnp.int32),
            pltpu.VMEM((1, tile_count), jnp.int32),
            dma((PHASES,)),
            dma((n,)),
            dma((n,)),
            dma((PHASES, n)),
            dma((PHASES, n)),
            dma((PHASES, CHUNKS, near)),
            dma((PHASES, CHUNKS, near)),
            dma((CHUNKS, n)),
            dma((CHUNKS, n)),
            dma((len(given),)),
        ],
        compiler_params=pltpu.CompilerParams(collective_id=0, has_side_effects=True, vmem_limit_bytes=BIG),
        name="flow",
    )(*[pltpu.with_memory_space_constraint(x, pltpu.MemorySpace.HBM) for x in given])


def solution(mesh):
    in_specs = (
        P(None, "date", "grp", None),
        P(None, "date", None),
        P("date"),
        P(),
        P(("grp", "date"), None),
        P(("grp", "date")),
        P(("grp", "date")),
        P(("grp", "date")),
    )
    out_specs = P(("grp", "date"), None, None)
    return jax.shard_map(
        partial(shards, mesh.shape["date"]), mesh=mesh, in_specs=in_specs, out_specs=out_specs, check_vma=False
    )
```

time: 80.2 us -> 83.6 us (1.042)
  Pallas kernels: 79.1 us -> 82.5 us
    pallas_call x1, Pallas kernels: 79.1 us -> 82.5 us  [shards(): pl.pallas_call(partial(flow_kernel, n), out_shape=jax.ShapeDtypeStruct((M...]
where the time goes in v1:
time: 83.6 us; the launch traced here: 83.5 us
  Pallas kernels  82.5 us (99%)
  local copies, waits for them, and re-layouts  0.97 us (1%)
    pallas_call x1, Pallas kernels, shards(): pl.pallas_call(partial(flow_kernel, n), out_shape=jax.ShapeDtypeStruct((M...  82.5 us

profile of v1, /device:TPU:0, one launch (start us, length us, event | category | flops | bytes accessed | tf_op | source)
XLA Modules:
  0.0 83.5 jit_solution(3306985978521753065)
XLA Ops:
  0.0 82.5 %flow.1 = f32[8,256,128]{2,1,0:T(8,128)S(1)} custom-call(s32[8]{0:T(128)} %refs_0_.1, f32[4]{0:T(128)} %refs_1_.1, bf16[2,8,128,256]{3,2,1,0:T(8,128)(2,1)} %refs_2_.1, f32[2,8,128]{2,1,0:T(8,128)} %refs_3_.1, s32[1,16]{1,0:T(1,128)} %bitcast.4, s32[1,16]{1,0:T(1,128)} %bitcast.5, s32[1,16]{1,0:T(1,128)} %bitcast.6, s32[1,16]{1,0:T(1,128)} %bitcast.7), custom_call_target="tpu_custom_call" | custom-call | tf_op jit(solution)/shard_map/flow/pallas_call | solution.py:341
  82.5 1.0 %copy.10 = f32[8,256,128]{2,1,0:T(8,128)} copy(f32[8,256,128]{2,1,0:T(8,128)S(1)} %flow.1) | data formatting | bytes 2097152

commit v2 on v1

v2 whole, which is shorter than its diff:
```python
from functools import partial

import jax
import jax.numpy as jnp
from jax import lax
from jax.experimental import pallas as pl
from jax.experimental.pallas import tpu as pltpu
from jax.sharding import PartitionSpec as P

PATCH_AZ = 8
PATCH_RG = 16
TILE = 128
KW = 4
MAP_DEV = 8
LANES = 128
PHASES = 2
TOGETHER = 4
SWEEPS = 3
GROUPS = 2
CHUNKS = 4
FACTS = 8
PAIR = 2 * PATCH_AZ

diag_load = 0.5
small_eps = 1e-05
MESH = pl.DeviceIdType.MESH
VMEM = pl.BlockSpec(memory_space=pltpu.VMEM)
HBM = pl.BlockSpec(memory_space=pltpu.MemorySpace.HBM)
BIG = 32 * 1024 * 1024


def across(x, y):
    return lax.dot_general(x, y, (((0,), (0,)), ((), ())), preferred_element_type=jnp.float32)


def operator_of(top):
    dates = top.shape[0]
    return jnp.concatenate([top, jnp.concatenate([-top[:, dates:], top[:, :dates]], axis=1)], axis=0)


def whiten_windows(z_ref, first, white_ref, half_ref, cells_ref, left_ref, right_ref):
    looks, dates = z_ref.shape[1], z_ref.shape[2] // 2
    eye = lax.broadcasted_iota(jnp.int32, (dates, dates), 0) == lax.broadcasted_iota(jnp.int32, (dates, dates), 1)
    overs = []
    for q in range(TOGETHER):
        zt = z_ref[first + q]
        zt_re, zt_im = zt[:, :dates], zt[:, dates:]
        top = across(
            jnp.concatenate([zt_re, zt_im], axis=0),
            jnp.concatenate([zt, jnp.concatenate([zt_im, -zt_re], axis=1)], axis=0),
        )
        diagonal = jnp.where(eye, top[:, :dates], 0.0)
        scale_col = lax.rsqrt(jnp.sum(diagonal, axis=1, keepdims=True) * (1.0 / looks) + small_eps) * (1.0 / looks)
        scale_row = lax.rsqrt(jnp.sum(diagonal, axis=0, keepdims=True) * (1.0 / looks) + small_eps)
        outer = scale_col * scale_row
        coher_re = top[:, :dates] * outer + jnp.where(eye, diag_load, 0.0)
        coher_im = top[:, dates:] * outer
        sums = jnp.sum(jnp.abs(coher_re) + jnp.abs(coher_im), axis=0, keepdims=True)
        over = 1.0 / jnp.max(sums, axis=1, keepdims=True)
        half = jnp.concatenate([coher_re, coher_im], axis=1) * (0.5 * over)
        half_ref[q] = half
        rounded = half.astype(jnp.bfloat16)
        left_ref[q] = jnp.concatenate([rounded, zt], axis=0)
        right_ref[q] = operator_of(rounded)
        overs.append(over)
    for stage in range(SWEEPS - 1):
        for q in range(TOGETHER):
            both = jnp.dot(left_ref[q], right_ref[q], preferred_element_type=jnp.float32)
            half = half_ref[q] - both[:dates]
            if stage == 0:
                cells = z_ref[first + q].astype(jnp.float32) - both[dates:]
            else:
                cells = cells_ref[q] - both[dates:]
            rounded = half.astype(jnp.bfloat16)
            if stage < SWEEPS - 2:
                half_ref[q] = half
                left_ref[q, :dates] = rounded
            cells_ref[q] = cells
            left_ref[q, dates:] = cells.astype(jnp.bfloat16)
            right_ref[q] = operator_of(rounded * (2.0 ** (stage + 1)))
    for q in range(TOGETHER):
        applied = jnp.dot(left_ref[q, dates:], right_ref[q], preferred_element_type=jnp.float32)
        white = ((cells_ref[q] - applied) * (2.0**SWEEPS * overs[q])).astype(jnp.bfloat16)
        for a in range(PATCH_AZ):
            white_ref[a, pl.ds((first + q) * PATCH_RG, PATCH_RG), :] = white[a * PATCH_RG : (a + 1) * PATCH_RG]


def flow_kernel(n, *refs):
    inputs, refs = refs[:8], refs[8:]
    result_ref, cells_ref, got_cells, facts_ref, got_facts, cell_ref, z_ref, white_ref, flat_ref = refs[:9]
    row_msg, got_rows, sum_msg, got_sums, operator_ref, spread_ref, shift_ref, inv_ref = refs[9:17]
    work, local, refs = refs[17:21], refs[21:29], refs[29:]
    len_ref, kern_ref, radar_ref, taps_ref = local[:4]
    fact_refs = local[4:8]
    own_sem, fact_send, fact_recv, cell_send, cell_recv, row_send, row_recv, sum_send, sum_recv, load_sem = refs
    me = lax.axis_index("date")
    dates_here, rows = radar_ref.shape[1], radar_ref.shape[2]
    taps, tile_count = taps_ref.shape[2], fact_refs[0].shape[1]
    total = n * dates_here
    windows = LANES // PATCH_RG
    near = n // GROUPS
    group, rank = me // near, me % near
    slots = spread_ref.shape[1]
    deep = 2 * total // near // CHUNKS

    barrier = pltpu.get_barrier_semaphore()
    loads = [pltpu.make_async_copy(x, y, load_sem.at[i]) for i, (x, y) in enumerate(zip(inputs, local))]
    for load in loads:
        load.start()
    for k in range(1, n):
        pl.semaphore_signal(barrier, inc=1, device_id={"date": lax.rem(me + k, n)}, device_id_type=MESH)
    own = [pltpu.make_async_copy(cells_ref.at[h, me], got_cells.at[h, me], own_sem.at[h]) for h in range(PHASES)]

    def send(src, dst, send_sem, recv_sem, peer):
        pltpu.make_async_remote_copy(
            src_ref=src,
            dst_ref=dst,
            send_sem=send_sem,
            recv_sem=recv_sem,
            device_id={"date": peer},
            device_id_type=MESH,
        ).start()

    def drain(ref, sem):
        pltpu.make_async_copy(ref, ref, sem).wait()

    def partner(k):
        peer, bit = me, 1
        while bit < n:
            peer = peer + (k // bit) % 2 * (1 - (me // bit) % 2 * 2) * bit
            bit *= 2
        return peer

    def turn(i):
        return n - 1 - i // 2 - i % 2 * (n // 2)

    peers = [turn(i) for i in range(n - 1)]
    inner = list(range(near - 1, 0, -1))

    for load in loads:
        load.wait()
    position = lax.broadcasted_iota(jnp.int32, (1, taps), 1)
    a_iota = lax.broadcasted_iota(jnp.int32, (rows, rows), 0)
    b_iota = lax.broadcasted_iota(jnp.int32, (rows, rows), 1)
    tap_at = b_iota - a_iota + taps // 2
    inside = jnp.logical_and(tap_at >= 0, tap_at < taps)

    def toeplitz(d, which):
        kept = jnp.where(position < len_ref[d], taps_ref[which, pl.ds(d, 1), :], 0.0)
        rolled = pltpu.roll(jnp.broadcast_to(kept, (rows, taps)), taps // 2, 1, stride=1, stride_axis=0)
        return jnp.where(inside, jnp.concatenate([rolled] * (rows // taps), axis=1), 0.0)

    for h in range(PHASES):
        for d in range(dates_here):
            if h == 0:
                t_re, t_im = toeplitz(d, 0), toeplitz(d, 1)
                operator_ref[d] = jnp.concatenate(
                    [jnp.concatenate([t_re, -t_im], axis=1), jnp.concatenate([t_im, t_re], axis=1)], axis=0
                ).astype(jnp.bfloat16)
            side = slice(h * LANES, (h + 1) * LANES)
            columns = jnp.concatenate([radar_ref[0, d, :, side], radar_ref[1, d, :, side]], axis=0)
            product = jnp.dot(operator_ref[d], columns, preferred_element_type=jnp.float32)
            for p in range(n):
                for part in range(2):
                    top = part * rows + p * PATCH_AZ
                    cell_ref[p, pl.ds(part * PATCH_AZ * dates_here + d, PATCH_AZ, stride=dates_here), :] = product[
                        top : top + PATCH_AZ
                    ]
        for p in range(n):
            cells_ref[h, p] = cell_ref[p].astype(jnp.bfloat16)
        if h == 0:
            pl.semaphore_wait(barrier, n - 1)
        for k in peers:
            send(cells_ref.at[h, partner(k)], got_cells.at[h, me], cell_send.at[0], cell_recv.at[h], partner(k))
        own[h].start()

    tile_at = lax.broadcasted_iota(jnp.int32, (LANES, slots), 0)
    lane_at = lax.broadcasted_iota(jnp.int32, (LANES, slots), 1)
    placed = ((tile_at & 1) * near + rank) * PAIR + (tile_at >> 1)
    hit = jnp.logical_or(lane_at == placed, lane_at == placed + PATCH_AZ)
    moving = jnp.where(jnp.logical_and(hit, tile_at < tile_count), 1.0, 0.0).astype(jnp.bfloat16)
    listed = jnp.concatenate([fact[...] for fact in fact_refs], axis=0).astype(jnp.float32)
    listed = jnp.concatenate([listed, jnp.zeros((FACTS - len(fact_refs), tile_count), jnp.float32)], axis=0)
    listed = jnp.concatenate([listed, jnp.zeros((FACTS, LANES - tile_count), jnp.float32)], axis=1)
    facts_ref[...] = jnp.dot(listed.astype(jnp.bfloat16), moving, preferred_element_type=jnp.float32)
    for k in peers:
        send(facts_ref, got_facts.at[me], fact_send.at[0], fact_recv.at[0], partner(k))
    got_facts[me] = facts_ref[...]

    apart = lax.broadcasted_iota(jnp.int32, (TILE, TILE), 0) - lax.broadcasted_iota(jnp.int32, (TILE, TILE), 1) + TILE
    for t in range(tile_count):
        shift = fact_refs[2][:, t : t + 1]
        shift_ref[t] = jnp.where(((apart - shift) & (TILE - 1)) == 0, 1.0, 0.0).astype(jnp.bfloat16)

    drain(got_facts.at[pl.ds(0, n - 1)], fact_recv.at[0])
    here = got_facts[group * near]
    for s in range(1, near):
        here = here + got_facts[group * near + s]
    row_at = lax.broadcasted_iota(jnp.int32, spread_ref.shape, 0)
    slot_at = lax.broadcasted_iota(jnp.int32, spread_ref.shape, 1)
    named = ((row_at >> 4) * MAP_DEV + (row_at & 7)).astype(jnp.float32)
    same = jnp.logical_and(named == here[0:1] * MAP_DEV + here[1:2], ((row_at ^ slot_at) & PATCH_AZ) == 0)
    spread_ref[...] = jnp.where(same, here[3:4], 0.0).astype(jnp.bfloat16)
    mine = (me * MAP_DEV + lax.broadcasted_iota(jnp.int32, (MAP_DEV, slots), 0)).astype(jnp.float32)
    once = (lax.broadcasted_iota(jnp.int32, (MAP_DEV, slots), 1) & PATCH_AZ) == 0
    count = jnp.zeros((MAP_DEV, slots), jnp.float32)
    for k in range(GROUPS):
        facts = got_facts[k * near]
        for s in range(1, near):
            facts = facts + got_facts[k * near + s]
        owned = jnp.logical_and(mine == facts[0:1] * MAP_DEV + facts[1:2], once)
        count = count + jnp.where(owned, facts[3:4], 0.0)
    inv_ref[...] = jnp.broadcast_to(1.0 / jnp.maximum(jnp.sum(count, axis=1, keepdims=True), 1.0), inv_ref.shape)

    for h in range(PHASES):
        own[h].wait()
        drain(got_cells.at[h, pl.ds(0, n - 1)], cell_recv.at[h])
        for s in range(n):
            cell_ref[s] = got_cells[h, s].astype(jnp.float32)
        for part in range(2):
            for a in range(PATCH_AZ):
                at = pl.ds((part * PATCH_AZ + a) * dates_here, dates_here)
                line = jnp.concatenate([cell_ref[s, at, :] for s in range(n)], axis=0).T.astype(jnp.bfloat16)
                for j in range(windows):
                    z_ref[j, a * PATCH_RG : (a + 1) * PATCH_RG, part * total : (part + 1) * total] = line[
                        j * PATCH_RG : (j + 1) * PATCH_RG
                    ]

        def whiten(i, carry):
            whiten_windows(z_ref, i * TOGETHER, white_ref, *work)
            return carry

        lax.fori_loop(0, windows // TOGETHER, whiten, 0)

        for a in range(PATCH_AZ):
            flat_ref[pl.ds(a, 2 * total, stride=PATCH_AZ), :] = across(white_ref[a], shift_ref[a * 2 + h])
        for q in range(CHUNKS):
            for to in range(near):
                row_msg[h, to, q] = flat_ref[
                    pl.ds((to * CHUNKS + q) * deep * PATCH_AZ, deep * PATCH_AZ), :
                ].astype(jnp.bfloat16)
            got_rows[h, rank, q] = row_msg[h, rank, q]
            if h == PHASES - 1:
                for k in inner:
                    to = partner(k) % near
                    send(row_msg.at[h, to, q], got_rows.at[h, rank, q], row_send.at[0], row_recv.at[1 + q], partner(k))
        if h < PHASES - 1:
            for k in inner:
                to = partner(k) % near
                send(row_msg.at[h, to], got_rows.at[h, rank], row_send.at[0], row_recv.at[0], partner(k))

    drain(got_rows.at[0, pl.ds(0, near - 1)], row_recv.at[0])

    def reduce(q, carry):
        drain(got_rows.at[1, pl.ds(0, near - 1), q], row_recv.at[1 + q])
        for i in range(deep // 2):
            at = slice(i * PAIR, (i + 1) * PAIR)
            cells = jnp.concatenate([got_rows[h, s, q, at, :] for h in range(PHASES) for s in range(near)], axis=0)
            out = jnp.dot(spread_ref[...], cells, preferred_element_type=jnp.float32).astype(jnp.bfloat16)
            for o in range(n):
                sum_msg[q, o, at, :] = out[o * PAIR : (o + 1) * PAIR]
        got_sums[q, me] = sum_msg[q, me]
        for k in peers:
            send(sum_msg.at[q, partner(k)], got_sums.at[q, me], sum_send.at[0], sum_recv.at[q], partner(k))
        return carry

    lax.fori_loop(0, CHUNKS, reduce, 0)

    weights = [kern_ref[k].astype(jnp.bfloat16).astype(jnp.float32) for k in range(KW)]

    def finish(q, carry):
        drain(got_sums.at[q, pl.ds(0, n - 1)], sum_recv.at[q])

        def place(s, carry):
            y = got_sums[q, s].astype(jnp.float32)
            for k in range(1, GROUPS):
                y = y + got_sums[q, s + k * near].astype(jnp.float32)
            out = weights[0] * y
            for k in range(1, KW):
                out = out + weights[k] * pltpu.roll(y, LANES - k, 1)
            for r in range(deep):
                at = pl.ds((s * CHUNKS + q) * deep + r, MAP_DEV, stride=2 * total)
                result_ref[at, :] = out[r * MAP_DEV : (r + 1) * MAP_DEV] * inv_ref[...]
            return carry

        lax.fori_loop(0, near, place, 0)
        return carry

    lax.fori_loop(0, CHUNKS, finish, 0)

    drain(got_facts.at[pl.ds(0, n - 1)], fact_send.at[0])
    drain(cells_ref.at[:, pl.ds(0, n - 1)], cell_send.at[0])
    drain(row_msg.at[:, pl.ds(0, near - 1)], row_send.at[0])
    drain(sum_msg.at[:, pl.ds(0, n - 1)], sum_send.at[0])


def shards(n, radar_stack, filter_taps, filter_lengths, resample_kernel, tile_owner, map_slot, correlation, offsets):
    dates_here, rows, ranges = radar_stack.shape[1:]
    dates = n * dates_here
    tile_count = tile_owner.shape[0]
    near = n // GROUPS
    slots = PHASES * near * PAIR
    deep = 2 * dates // near // CHUNKS
    block = (PHASES, n, 2 * PATCH_AZ * dates_here, LANES)
    row_block = (PHASES, near, CHUNKS, deep * PATCH_AZ, LANES)
    sum_block = (CHUNKS, n, MAP_DEV * deep, LANES)
    facts = [x.reshape(1, tile_count) for x in (tile_owner, map_slot, offsets, correlation)]
    given = (filter_lengths, resample_kernel, radar_stack, filter_taps, *facts)

    dma = pltpu.SemaphoreType.DMA
    result = pl.pallas_call(
        partial(flow_kernel, n),
        out_shape=jax.ShapeDtypeStruct((MAP_DEV * 2 * dates, TILE), jnp.float32),
        in_specs=[HBM] * len(given),
        out_specs=VMEM,
        scratch_shapes=[
            pltpu.VMEM(block, jnp.bfloat16),
            pltpu.VMEM(block, jnp.bfloat16),
            pltpu.VMEM((FACTS, slots), jnp.float32),
            pltpu.VMEM((n, FACTS, slots), jnp.float32),
            pltpu.VMEM(block[1:], jnp.float32),
            pltpu.VMEM((LANES // PATCH_RG, LANES, 2 * dates), jnp.bfloat16),
            pltpu.VMEM((PATCH_AZ, LANES, 2 * dates), jnp.bfloat16),
            pltpu.VMEM((2 * dates * PATCH_AZ, LANES), jnp.float32),
            pltpu.VMEM(row_block, jnp.bfloat16),
            pltpu.VMEM(row_block, jnp.bfloat16),
            pltpu.VMEM(sum_block, jnp.bfloat16),
            pltpu.VMEM(sum_block, jnp.bfloat16),
            pltpu.VMEM((dates_here, 2 * rows, 2 * rows), jnp.bfloat16),
            pltpu.VMEM((n * PAIR, slots), jnp.bfloat16),
            pltpu.VMEM((tile_count, TILE, TILE), jnp.bfloat16),
            pltpu.VMEM((MAP_DEV, LANES), jnp.float32),
            pltpu.VMEM((TOGETHER, dates, 2 * dates), jnp.float32),
            pltpu.VMEM((TOGETHER, LANES, 2 * dates), jnp.float32),
            pltpu.VMEM((TOGETHER, dates + LANES, 2 * dates), jnp.bfloat16),
            pltpu.VMEM((TOGETHER, 2 * dates, 2 * dates), jnp.bfloat16),
            pltpu.SMEM(filter_lengths.shape, jnp.int32),
            pltpu.SMEM(resample_kernel.shape, jnp.float32),
            pltpu.VMEM(radar_stack.shape, radar_stack.dtype),
            pltpu.VMEM(filter_taps.shape, jnp.float32),
            pltpu.VMEM((1, tile_count), jnp.int32),
            pltpu.VMEM((1, tile_count), jnp.int32),
            pltpu.VMEM((1, tile_count), jnp.int32),
            pltpu.VMEM((1, tile_count), jnp.int32),
            dma((PHASES,)),
            dma((1,)),
            dma((1,)),
            dma((1,)),
            dma((PHASES,)),
            dma((1,)),
            dma((1 + CHUNKS,)),
            dma((1,)),
            dma((CHUNKS,)),
            dma((len(given),)),
        ],
        compiler_params=pltpu.CompilerParams(collective_id=0, has_side_effects=True, vmem_limit_bytes=BIG),
        name="flow",
    )(*[pltpu.with_memory_space_constraint(x, pltpu.MemorySpace.HBM) for x in given])
    return result.reshape(MAP_DEV, 2 * dates, TILE)


def solution(mesh):
    in_specs = (
        P(None, "date", "grp", None),
        P(None, "date", None),
        P("date"),
        P(),
        P(("grp", "date"), None),
        P(("grp", "date")),
        P(("grp", "date")),
        P(("grp", "date")),
    )
    out_specs = P(("grp", "date"), None, None)
    return jax.shard_map(
        partial(shards, mesh.shape["date"]), mesh=mesh, in_specs=in_specs, out_specs=out_specs, check_vma=False
    )
```

time: 83.6 us -> 73.6 us (0.88)
  Pallas kernels: 82.5 us -> 72.5 us
    pallas_call x1, Pallas kernels: 82.5 us -> 72.5 us  [shards(): pl.pallas_call(partial(flow_kernel, n), out_shape=jax.ShapeDtypeStruct((M...]
where the time goes in v2:
time: 73.6 us; the launch traced here: 73.5 us
  Pallas kernels  72.5 us (99%)
  local copies, waits for them, and re-layouts  0.97 us (1%)
    pallas_call x1, Pallas kernels, shards(): pl.pallas_call(partial(flow_kernel, n), out_shape=jax.ShapeDtypeStruct((M...  72.5 us

profile of v2, /device:TPU:0, one launch (start us, length us, event | category | flops | bytes accessed | tf_op | source)
XLA Modules:
  0.0 73.5 jit_solution(9144079260296147914)
XLA Ops:
  0.0 72.5 %flow.1 = f32[2048,128]{1,0:T(8,128)S(1)} custom-call(s32[8]{0:T(128)} %refs_0_.1, f32[4]{0:T(128)} %refs_1_.1, bf16[2,8,128,256]{3,2,1,0:T(8,128)(2,1)} %refs_2_.1, f32[2,8,128]{2,1,0:T(8,128)} %refs_3_.1, s32[1,16]{1,0:T(1,128)} %bitcast.6, s32[1,16]{1,0:T(1,128)} %bitcast.7, s32[1,16]{1,0:T(1,128)} %bitcast.8, s32[1,16]{1,0:T(1,128)} %bitcast.9), custom_call_target="tpu_custom_call" | custom-call | tf_op jit(solution)/shard_map/flow/pallas_call | solution.py:311
  72.5 1.0 %copy.10 = f32[8,256,128]{2,1,0:T(8,128)} copy(f32[8,256,128]{2,1,0:T(8,128)S(1)} %bitcast.5) | data formatting | bytes 2097152

commit v3 on v2

--- a/solution.py
+++ b/solution.py
@@ -139,6 +139,15 @@
 
     for load in loads:
         load.wait()
+    tile_at = lax.broadcasted_iota(jnp.int32, (LANES, slots), 0)
+    lane_at = lax.broadcasted_iota(jnp.int32, (LANES, slots), 1)
+    placed = ((tile_at & 1) * near + rank) * PAIR + (tile_at >> 1)
+    hit = jnp.logical_or(lane_at == placed, lane_at == placed + PATCH_AZ)
+    moving = jnp.where(jnp.logical_and(hit, tile_at < tile_count), 1.0, 0.0).astype(jnp.bfloat16)
+    listed = jnp.concatenate([fact[...] for fact in fact_refs], axis=0).astype(jnp.float32)
+    listed = jnp.concatenate([listed, jnp.zeros((FACTS - len(fact_refs), tile_count), jnp.float32)], axis=0)
+    listed = jnp.concatenate([listed, jnp.zeros((FACTS, LANES - tile_count), jnp.float32)], axis=1)
+    facts_ref[...] = jnp.dot(listed.astype(jnp.bfloat16), moving, preferred_element_type=jnp.float32)
     position = lax.broadcasted_iota(jnp.int32, (1, taps), 1)
     a_iota = lax.broadcasted_iota(jnp.int32, (rows, rows), 0)
     b_iota = lax.broadcasted_iota(jnp.int32, (rows, rows), 1)
@@ -170,47 +179,38 @@
             cells_ref[h, p] = cell_ref[p].astype(jnp.bfloat16)
         if h == 0:
             pl.semaphore_wait(barrier, n - 1)
+            for k in peers:
+                send(facts_ref, got_facts.at[me], fact_send.at[0], fact_recv.at[0], partner(k))
+            got_facts[me] = facts_ref[...]
         for k in peers:
             send(cells_ref.at[h, partner(k)], got_cells.at[h, me], cell_send.at[0], cell_recv.at[h], partner(k))
         own[h].start()
-
-    tile_at = lax.broadcasted_iota(jnp.int32, (LANES, slots), 0)
-    lane_at = lax.broadcasted_iota(jnp.int32, (LANES, slots), 1)
-    placed = ((tile_at & 1) * near + rank) * PAIR + (tile_at >> 1)
-    hit = jnp.logical_or(lane_at == placed, lane_at == placed + PATCH_AZ)
-    moving = jnp.where(jnp.logical_and(hit, tile_at < tile_count), 1.0, 0.0).astype(jnp.bfloat16)
-    listed = jnp.concatenate([fact[...] for fact in fact_refs], axis=0).astype(jnp.float32)
-    listed = jnp.concatenate([listed, jnp.zeros((FACTS - len(fact_refs), tile_count), jnp.float32)], axis=0)
-    listed = jnp.concatenate([listed, jnp.zeros((FACTS, LANES - tile_count), jnp.float32)], axis=1)
-    facts_ref[...] = jnp.dot(listed.astype(jnp.bfloat16), moving, preferred_element_type=jnp.float32)
-    for k in peers:
-        send(facts_ref, got_facts.at[me], fact_send.at[0], fact_recv.at[0], partner(k))
-    got_facts[me] = facts_ref[...]
 
     apart = lax.broadcasted_iota(jnp.int32, (TILE, TILE), 0) - lax.broadcasted_iota(jnp.int32, (TILE, TILE), 1) + TILE
     for t in range(tile_count):
         shift = fact_refs[2][:, t : t + 1]
         shift_ref[t] = jnp.where(((apart - shift) & (TILE - 1)) == 0, 1.0, 0.0).astype(jnp.bfloat16)
 
-    drain(got_facts.at[pl.ds(0, n - 1)], fact_recv.at[0])
-    here = got_facts[group * near]
-    for s in range(1, near):
-        here = here + got_facts[group * near + s]
-    row_at = lax.broadcasted_iota(jnp.int32, spread_ref.shape, 0)
-    slot_at = lax.broadcasted_iota(jnp.int32, spread_ref.shape, 1)
-    named = ((row_at >> 4) * MAP_DEV + (row_at & 7)).astype(jnp.float32)
-    same = jnp.logical_and(named == here[0:1] * MAP_DEV + here[1:2], ((row_at ^ slot_at) & PATCH_AZ) == 0)
-    spread_ref[...] = jnp.where(same, here[3:4], 0.0).astype(jnp.bfloat16)
-    mine = (me * MAP_DEV + lax.broadcasted_iota(jnp.int32, (MAP_DEV, slots), 0)).astype(jnp.float32)
-    once = (lax.broadcasted_iota(jnp.int32, (MAP_DEV, slots), 1) & PATCH_AZ) == 0
-    count = jnp.zeros((MAP_DEV, slots), jnp.float32)
-    for k in range(GROUPS):
-        facts = got_facts[k * near]
+    def settle():
+        drain(got_facts.at[pl.ds(0, n - 1)], fact_recv.at[0])
+        here = got_facts[group * near]
         for s in range(1, near):
-            facts = facts + got_facts[k * near + s]
-        owned = jnp.logical_and(mine == facts[0:1] * MAP_DEV + facts[1:2], once)
-        count = count + jnp.where(owned, facts[3:4], 0.0)
-    inv_ref[...] = jnp.broadcast_to(1.0 / jnp.maximum(jnp.sum(count, axis=1, keepdims=True), 1.0), inv_ref.shape)
+            here = here + got_facts[group * near + s]
+        row_at = lax.broadcasted_iota(jnp.int32, spread_ref.shape, 0)
+        slot_at = lax.broadcasted_iota(jnp.int32, spread_ref.shape, 1)
+        named = ((row_at >> 4) * MAP_DEV + (row_at & 7)).astype(jnp.float32)
+        same = jnp.logical_and(named == here[0:1] * MAP_DEV + here[1:2], ((row_at ^ slot_at) & PATCH_AZ) == 0)
+        spread_ref[...] = jnp.where(same, here[3:4], 0.0).astype(jnp.bfloat16)
+        mine = (me * MAP_DEV + lax.broadcasted_iota(jnp.int32, (MAP_DEV, slots), 0)).astype(jnp.float32)
+        once = (lax.broadcasted_iota(jnp.int32, (MAP_DEV, slots), 1) & PATCH_AZ) == 0
+        count = jnp.zeros((MAP_DEV, slots), jnp.float32)
+        for k in range(GROUPS):
+            facts = got_facts[k * near]
+            for s in range(1, near):
+                facts = facts + got_facts[k * near + s]
+            owned = jnp.logical_and(mine == facts[0:1] * MAP_DEV + facts[1:2], once)
+            count = count + jnp.where(owned, facts[3:4], 0.0)
+        inv_ref[...] = jnp.broadcast_to(1.0 / jnp.maximum(jnp.sum(count, axis=1, keepdims=True), 1.0), inv_ref.shape)
 
     for h in range(PHASES):
         own[h].wait()
@@ -248,6 +248,7 @@
             for k in inner:
                 to = partner(k) % near
                 send(row_msg.at[h, to], got_rows.at[h, rank], row_send.at[0], row_recv.at[0], partner(k))
+            settle()
 
     drain(got_rows.at[0, pl.ds(0, near - 1)], row_recv.at[0])
 

time: 73.6 us -> 67.3 us (0.914)
  Pallas kernels: 72.5 us -> 66.2 us
    pallas_call x1, Pallas kernels: 72.5 us -> 66.2 us  [shards(): pl.pallas_call(partial(flow_kernel, n), out_shape=jax.ShapeDtypeStruct((M...]
where the time goes in v3:
time: 67.3 us; the launch traced here: 67.2 us
  Pallas kernels  66.2 us (98%)
  local copies, waits for them, and re-layouts  0.97 us (1%)
    pallas_call x1, Pallas kernels, shards(): pl.pallas_call(partial(flow_kernel, n), out_shape=jax.ShapeDtypeStruct((M...  66.2 us

profile of v3, /device:TPU:0, one launch (start us, length us, event | category | flops | bytes accessed | tf_op | source)
XLA Modules:
  0.0 67.2 jit_solution(15711301412749994619)
XLA Ops:
  0.0 66.2 %flow.1 = f32[2048,128]{1,0:T(8,128)S(1)} custom-call(s32[8]{0:T(128)} %refs_0_.1, f32[4]{0:T(128)} %refs_1_.1, bf16[2,8,128,256]{3,2,1,0:T(8,128)(2,1)} %refs_2_.1, f32[2,8,128]{2,1,0:T(8,128)} %refs_3_.1, s32[1,16]{1,0:T(1,128)} %bitcast.6, s32[1,16]{1,0:T(1,128)} %bitcast.7, s32[1,16]{1,0:T(1,128)} %bitcast.8, s32[1,16]{1,0:T(1,128)} %bitcast.9), custom_call_target="tpu_custom_call" | custom-call | tf_op jit(solution)/shard_map/flow/pallas_call | solution.py:312
  66.2 1.0 %copy.10 = f32[8,256,128]{2,1,0:T(8,128)} copy(f32[8,256,128]{2,1,0:T(8,128)S(1)} %bitcast.5) | data formatting | bytes 2097152

commit v4 on v3

--- a/solution.py
+++ b/solution.py
@@ -17,7 +17,7 @@
 TOGETHER = 4
 SWEEPS = 3
 GROUPS = 2
-CHUNKS = 4
+CHUNKS = 8
 FACTS = 8
 PAIR = 2 * PATCH_AZ
 
@@ -87,9 +87,9 @@
 
 def flow_kernel(n, *refs):
     inputs, refs = refs[:8], refs[8:]
-    result_ref, cells_ref, got_cells, facts_ref, got_facts, cell_ref, z_ref, white_ref, flat_ref = refs[:9]
-    row_msg, got_rows, sum_msg, got_sums, operator_ref, spread_ref, shift_ref, inv_ref = refs[9:17]
-    work, local, refs = refs[17:21], refs[21:29], refs[29:]
+    result_ref, cells_ref, got_cells, split_ref, got_split, facts_ref, got_facts, cell_ref, z_ref, white_ref, flat_ref = refs[:11]
+    row_msg, got_rows, sum_msg, got_sums, operator_ref, spread_ref, shift_ref, inv_ref = refs[11:19]
+    work, local, refs = refs[19:23], refs[23:31], refs[31:]
     len_ref, kern_ref, radar_ref, taps_ref = local[:4]
     fact_refs = local[4:8]
     own_sem, fact_send, fact_recv, cell_send, cell_recv, row_send, row_recv, sum_send, sum_recv, load_sem = refs
@@ -109,7 +109,8 @@
         load.start()
     for k in range(1, n):
         pl.semaphore_signal(barrier, inc=1, device_id={"date": lax.rem(me + k, n)}, device_id_type=MESH)
-    own = [pltpu.make_async_copy(cells_ref.at[h, me], got_cells.at[h, me], own_sem.at[h]) for h in range(PHASES)]
+    own = [pltpu.make_async_copy(cells_ref.at[me], got_cells.at[me], own_sem.at[0])]
+    own += [pltpu.make_async_copy(split_ref.at[u, me], got_split.at[u, me], own_sem.at[1 + u]) for u in range(2)]
 
     def send(src, dst, send_sem, recv_sem, peer):
         pltpu.make_async_remote_copy(
@@ -175,21 +176,38 @@
                     cell_ref[p, pl.ds(part * PATCH_AZ * dates_here + d, PATCH_AZ, stride=dates_here), :] = product[
                         top : top + PATCH_AZ
                     ]
-        for p in range(n):
-            cells_ref[h, p] = cell_ref[p].astype(jnp.bfloat16)
         if h == 0:
+            for p in range(n):
+                cells_ref[p] = cell_ref[p].astype(jnp.bfloat16)
             pl.semaphore_wait(barrier, n - 1)
             for k in peers:
                 send(facts_ref, got_facts.at[me], fact_send.at[0], fact_recv.at[0], partner(k))
             got_facts[me] = facts_ref[...]
-        for k in peers:
-            send(cells_ref.at[h, partner(k)], got_cells.at[h, me], cell_send.at[0], cell_recv.at[h], partner(k))
-        own[h].start()
+            for k in peers:
+                send(cells_ref.at[partner(k)], got_cells.at[me], cell_send.at[0], cell_recv.at[0], partner(k))
+            own[0].start()
+        else:
+            low = lax.broadcasted_iota(jnp.int32, (PATCH_AZ * dates_here, LANES), 1) < LANES // 2
+            for p in range(n):
+                lines = cell_ref[p].reshape(PATCH_AZ, 2, dates_here, LANES)
+                even, odd = [lines[:, i].reshape(PATCH_AZ * dates_here, LANES) for i in range(2)]
+                split_ref[0, p] = jnp.where(low, even, pltpu.roll(odd, LANES // 2, 1)).astype(jnp.bfloat16)
+                split_ref[1, p] = jnp.where(low, pltpu.roll(even, LANES // 2, 1), odd).astype(jnp.bfloat16)
+            for u in range(2):
+                for k in peers:
+                    send(
+                        split_ref.at[u, partner(k)], got_split.at[u, me], cell_send.at[1], cell_recv.at[1 + u], partner(k)
+                    )
+                own[1 + u].start()
 
     apart = lax.broadcasted_iota(jnp.int32, (TILE, TILE), 0) - lax.broadcasted_iota(jnp.int32, (TILE, TILE), 1) + TILE
     for t in range(tile_count):
         shift = fact_refs[2][:, t : t + 1]
-        shift_ref[t] = jnp.where(((apart - shift) & (TILE - 1)) == 0, 1.0, 0.0).astype(jnp.bfloat16)
+        step = (apart - shift) & (TILE - 1)
+        circ = jnp.zeros((TILE, TILE), jnp.float32)
+        for k in range(KW):
+            circ = jnp.where(step == k, kern_ref[k], circ)
+        shift_ref[t] = circ.astype(jnp.bfloat16)
 
     def settle():
         drain(got_facts.at[pl.ds(0, n - 1)], fact_recv.at[0])
@@ -212,25 +230,47 @@
             count = count + jnp.where(owned, facts[3:4], 0.0)
         inv_ref[...] = jnp.broadcast_to(1.0 / jnp.maximum(jnp.sum(count, axis=1, keepdims=True), 1.0), inv_ref.shape)
 
+    def whiten(i, carry):
+        whiten_windows(z_ref, i * TOGETHER, white_ref, *work)
+        return carry
+
+    def line_of(at):
+        return jnp.concatenate([cell_ref[s, at, :] for s in range(n)], axis=0).T.astype(jnp.bfloat16)
+
     for h in range(PHASES):
-        own[h].wait()
-        drain(got_cells.at[h, pl.ds(0, n - 1)], cell_recv.at[h])
-        for s in range(n):
-            cell_ref[s] = got_cells[h, s].astype(jnp.float32)
-        for part in range(2):
-            for a in range(PATCH_AZ):
-                at = pl.ds((part * PATCH_AZ + a) * dates_here, dates_here)
-                line = jnp.concatenate([cell_ref[s, at, :] for s in range(n)], axis=0).T.astype(jnp.bfloat16)
-                for j in range(windows):
-                    z_ref[j, a * PATCH_RG : (a + 1) * PATCH_RG, part * total : (part + 1) * total] = line[
-                        j * PATCH_RG : (j + 1) * PATCH_RG
-                    ]
-
-        def whiten(i, carry):
-            whiten_windows(z_ref, i * TOGETHER, white_ref, *work)
-            return carry
-
-        lax.fori_loop(0, windows // TOGETHER, whiten, 0)
+        if h == 0:
+            own[0].wait()
+            drain(got_cells.at[pl.ds(0, n - 1)], cell_recv.at[0])
+            for s in range(n):
+                cell_ref[s] = got_cells[s].astype(jnp.float32)
+            for part in range(2):
+                for a in range(PATCH_AZ):
+                    line = line_of(pl.ds((part * PATCH_AZ + a) * dates_here, dates_here))
+                    for j in range(windows):
+                        z_ref[j, a * PATCH_RG : (a + 1) * PATCH_RG, part * total : (part + 1) * total] = line[
+                            j * PATCH_RG : (j + 1) * PATCH_RG
+                        ]
+            lax.fori_loop(0, windows // TOGETHER, whiten, 0)
+        else:
+            for u in range(2):
+                own[1 + u].wait()
+                drain(got_split.at[u, pl.ds(0, n - 1)], cell_recv.at[1 + u])
+                for s in range(n):
+                    cell_ref[s, : PATCH_AZ * dates_here] = got_split[u, s].astype(jnp.float32)
+                for part in range(2):
+                    for b in range(PATCH_AZ // 2):
+                        line = line_of(pl.ds((part * (PATCH_AZ // 2) + b) * dates_here, dates_here))
+                        for i in range(2):
+                            a = 2 * b + i
+                            for j in range(windows // 2):
+                                at = i * (LANES // 2) + j * PATCH_RG
+                                z_ref[
+                                    u * (windows // 2) + j,
+                                    a * PATCH_RG : (a + 1) * PATCH_RG,
+                                    part * total : (part + 1) * total,
+                                ] = line[at : at + PATCH_RG]
+                for i in range(windows // 2 // TOGETHER):
+                    whiten(u * (windows // 2 // TOGETHER) + i, 0)
 
         for a in range(PATCH_AZ):
             flat_ref[pl.ds(a, 2 * total, stride=PATCH_AZ), :] = across(white_ref[a], shift_ref[a * 2 + h])
@@ -267,30 +307,23 @@
 
     lax.fori_loop(0, CHUNKS, reduce, 0)
 
-    weights = [kern_ref[k].astype(jnp.bfloat16).astype(jnp.float32) for k in range(KW)]
-
     def finish(q, carry):
         drain(got_sums.at[q, pl.ds(0, n - 1)], sum_recv.at[q])
 
-        def place(s, carry):
+        for s in range(near):
             y = got_sums[q, s].astype(jnp.float32)
             for k in range(1, GROUPS):
                 y = y + got_sums[q, s + k * near].astype(jnp.float32)
-            out = weights[0] * y
-            for k in range(1, KW):
-                out = out + weights[k] * pltpu.roll(y, LANES - k, 1)
             for r in range(deep):
                 at = pl.ds((s * CHUNKS + q) * deep + r, MAP_DEV, stride=2 * total)
-                result_ref[at, :] = out[r * MAP_DEV : (r + 1) * MAP_DEV] * inv_ref[...]
-            return carry
-
-        lax.fori_loop(0, near, place, 0)
+                result_ref[at, :] = y[r * MAP_DEV : (r + 1) * MAP_DEV] * inv_ref[...]
         return carry
 
     lax.fori_loop(0, CHUNKS, finish, 0)
 
     drain(got_facts.at[pl.ds(0, n - 1)], fact_send.at[0])
-    drain(cells_ref.at[:, pl.ds(0, n - 1)], cell_send.at[0])
+    drain(cells_ref.at[pl.ds(0, n - 1)], cell_send.at[0])
+    drain(split_ref.at[:, pl.ds(0, n - 1)], cell_send.at[1])
     drain(row_msg.at[:, pl.ds(0, near - 1)], row_send.at[0])
     drain(sum_msg.at[:, pl.ds(0, n - 1)], sum_send.at[0])
 
@@ -302,7 +335,8 @@
     near = n // GROUPS
     slots = PHASES * near * PAIR
     deep = 2 * dates // near // CHUNKS
-    block = (PHASES, n, 2 * PATCH_AZ * dates_here, LANES)
+    block = (n, 2 * PATCH_AZ * dates_here, LANES)
+    split = (2, n, PATCH_AZ * dates_here, LANES)
     row_block = (PHASES, near, CHUNKS, deep * PATCH_AZ, LANES)
     sum_block = (CHUNKS, n, MAP_DEV * deep, LANES)
     facts = [x.reshape(1, tile_count) for x in (tile_owner, map_slot, offsets, correlation)]
@@ -317,9 +351,11 @@
         scratch_shapes=[
             pltpu.VMEM(block, jnp.bfloat16),
             pltpu.VMEM(block, jnp.bfloat16),
+            pltpu.VMEM(split, jnp.bfloat16),
+            pltpu.VMEM(split, jnp.bfloat16),
             pltpu.VMEM((FACTS, slots), jnp.float32),
             pltpu.VMEM((n, FACTS, slots), jnp.float32),
-            pltpu.VMEM(block[1:], jnp.float32),
+            pltpu.VMEM(block, jnp.float32),
             pltpu.VMEM((LANES // PATCH_RG, LANES, 2 * dates), jnp.bfloat16),
             pltpu.VMEM((PATCH_AZ, LANES, 2 * dates), jnp.bfloat16),
             pltpu.VMEM((2 * dates * PATCH_AZ, LANES), jnp.float32),
@@ -343,11 +379,11 @@
             pltpu.VMEM((1, tile_count), jnp.int32),
             pltpu.VMEM((1, tile_count), jnp.int32),
             pltpu.VMEM((1, tile_count), jnp.int32),
-            dma((PHASES,)),
+            dma((3,)),
             dma((1,)),
             dma((1,)),
-            dma((1,)),
-            dma((PHASES,)),
+            dma((2,)),
+            dma((3,)),
             dma((1,)),
             dma((1 + CHUNKS,)),
             dma((1,)),

time: 67.3 us -> 65.2 us (0.969)
  Pallas kernels: 66.2 us -> 64 us
    pallas_call x1, Pallas kernels: 66.2 us -> 64 us  [shards(): pl.pallas_call(partial(flow_kernel, n), out_shape=jax.ShapeDtypeStruct((M...]
where the time goes in v4:
time: 65.2 us; the launch traced here: 65 us
  Pallas kernels  64 us (98%)
  local copies, waits for them, and re-layouts  0.97 us (1%)
    pallas_call x1, Pallas kernels, shards(): pl.pallas_call(partial(flow_kernel, n), out_shape=jax.ShapeDtypeStruct((M...  64 us

profile of v4, /device:TPU:0, one launch (start us, length us, event | category | flops | bytes accessed | tf_op | source)
XLA Modules:
  0.0 65.0 jit_solution(5448333755998604657)
XLA Ops:
  0.0 64.0 %flow.1 = f32[2048,128]{1,0:T(8,128)S(1)} custom-call(s32[8]{0:T(128)} %refs_0_.1, f32[4]{0:T(128)} %refs_1_.1, bf16[2,8,128,256]{3,2,1,0:T(8,128)(2,1)} %refs_2_.1, f32[2,8,128]{2,1,0:T(8,128)} %refs_3_.1, s32[1,16]{1,0:T(1,128)} %bitcast.6, s32[1,16]{1,0:T(1,128)} %bitcast.7, s32[1,16]{1,0:T(1,128)} %bitcast.8, s32[1,16]{1,0:T(1,128)} %bitcast.9), custom_call_target="tpu_custom_call" | custom-call | tf_op jit(solution)/shard_map/flow/pallas_call | solution.py:346
  64.0 1.0 %copy.10 = f32[8,256,128]{2,1,0:T(8,128)} copy(f32[8,256,128]{2,1,0:T(8,128)S(1)} %bitcast.5) | data formatting | bytes 2097152

commit v5 on v4

--- a/solution.py
+++ b/solution.py
@@ -18,6 +18,7 @@
 SWEEPS = 3
 GROUPS = 2
 CHUNKS = 8
+AHEAD = 2
 FACTS = 8
 PAIR = 2 * PATCH_AZ
 
@@ -140,15 +141,16 @@
 
     for load in loads:
         load.wait()
-    tile_at = lax.broadcasted_iota(jnp.int32, (LANES, slots), 0)
-    lane_at = lax.broadcasted_iota(jnp.int32, (LANES, slots), 1)
-    placed = ((tile_at & 1) * near + rank) * PAIR + (tile_at >> 1)
-    hit = jnp.logical_or(lane_at == placed, lane_at == placed + PATCH_AZ)
-    moving = jnp.where(jnp.logical_and(hit, tile_at < tile_count), 1.0, 0.0).astype(jnp.bfloat16)
-    listed = jnp.concatenate([fact[...] for fact in fact_refs], axis=0).astype(jnp.float32)
-    listed = jnp.concatenate([listed, jnp.zeros((FACTS - len(fact_refs), tile_count), jnp.float32)], axis=0)
-    listed = jnp.concatenate([listed, jnp.zeros((FACTS, LANES - tile_count), jnp.float32)], axis=1)
-    facts_ref[...] = jnp.dot(listed.astype(jnp.bfloat16), moving, preferred_element_type=jnp.float32)
+    tiles = slots // 2
+    tile_at = lax.broadcasted_iota(jnp.int32, (LANES, tiles), 0)
+    lane_at = lax.broadcasted_iota(jnp.int32, (LANES, tiles), 1)
+    placed = ((tile_at & 1) * near + rank) * PATCH_AZ + (tile_at >> 1)
+    hit = jnp.logical_and(lane_at == placed, tile_at < tile_count)
+    moving = jnp.where(hit, 1.0, 0.0).astype(jnp.bfloat16)
+    listed = jnp.concatenate([fact_refs[0][...] * MAP_DEV + fact_refs[1][...], fact_refs[3][...]], axis=0)
+    listed = jnp.concatenate([listed.astype(jnp.float32), jnp.zeros((2, LANES - tile_count), jnp.float32)], axis=1)
+    listed = jnp.concatenate([listed, jnp.zeros((FACTS - 2, LANES), jnp.float32)], axis=0)
+    facts_ref[...] = jnp.dot(listed.astype(jnp.bfloat16), moving, preferred_element_type=jnp.float32)[:2]
     position = lax.broadcasted_iota(jnp.int32, (1, taps), 1)
     a_iota = lax.broadcasted_iota(jnp.int32, (rows, rows), 0)
     b_iota = lax.broadcasted_iota(jnp.int32, (rows, rows), 1)
@@ -209,25 +211,40 @@
             circ = jnp.where(step == k, kern_ref[k], circ)
         shift_ref[t] = circ.astype(jnp.bfloat16)
 
+    def send_rows(q):
+        for k in inner:
+            to = partner(k) % near
+            send(row_msg.at[1, to, q], got_rows.at[1, rank, q], row_send.at[0], row_recv.at[1 + q], partner(k))
+
+    def send_sums(q, ks):
+        for k in ks:
+            send(sum_msg.at[q, partner(k)], got_sums.at[q, me], sum_send.at[0], sum_recv.at[q], partner(k))
+
     def settle():
         drain(got_facts.at[pl.ds(0, n - 1)], fact_recv.at[0])
-        here = got_facts[group * near]
-        for s in range(1, near):
-            here = here + got_facts[group * near + s]
+        from_at = lax.broadcasted_iota(jnp.int32, (tiles, slots), 0)
+        into_at = lax.broadcasted_iota(jnp.int32, (tiles, slots), 1)
+        twice = ((into_at >> 4) * PATCH_AZ + (into_at & (PATCH_AZ - 1))) == from_at
+        twice = jnp.where(twice, 1.0, 0.0).astype(jnp.bfloat16)
+
+        def all_of(k):
+            facts = got_facts[k * near]
+            for s in range(1, near):
+                facts = facts + got_facts[k * near + s]
+            return facts
+
+        here = jnp.concatenate([all_of(group), jnp.zeros((FACTS - 2, tiles), jnp.float32)], axis=0)
+        here = jnp.dot(here.astype(jnp.bfloat16), twice, preferred_element_type=jnp.float32)
         row_at = lax.broadcasted_iota(jnp.int32, spread_ref.shape, 0)
         slot_at = lax.broadcasted_iota(jnp.int32, spread_ref.shape, 1)
         named = ((row_at >> 4) * MAP_DEV + (row_at & 7)).astype(jnp.float32)
-        same = jnp.logical_and(named == here[0:1] * MAP_DEV + here[1:2], ((row_at ^ slot_at) & PATCH_AZ) == 0)
-        spread_ref[...] = jnp.where(same, here[3:4], 0.0).astype(jnp.bfloat16)
-        mine = (me * MAP_DEV + lax.broadcasted_iota(jnp.int32, (MAP_DEV, slots), 0)).astype(jnp.float32)
-        once = (lax.broadcasted_iota(jnp.int32, (MAP_DEV, slots), 1) & PATCH_AZ) == 0
-        count = jnp.zeros((MAP_DEV, slots), jnp.float32)
+        same = jnp.logical_and(named == here[0:1], ((row_at ^ slot_at) & PATCH_AZ) == 0)
+        spread_ref[...] = jnp.where(same, here[1:2], 0.0).astype(jnp.bfloat16)
+        mine = (me * MAP_DEV + lax.broadcasted_iota(jnp.int32, (MAP_DEV, tiles), 0)).astype(jnp.float32)
+        count = jnp.zeros((MAP_DEV, tiles), jnp.float32)
         for k in range(GROUPS):
-            facts = got_facts[k * near]
-            for s in range(1, near):
-                facts = facts + got_facts[k * near + s]
-            owned = jnp.logical_and(mine == facts[0:1] * MAP_DEV + facts[1:2], once)
-            count = count + jnp.where(owned, facts[3:4], 0.0)
+            facts = all_of(k)
+            count = count + jnp.where(mine == facts[0:1], facts[1:2], 0.0)
         inv_ref[...] = jnp.broadcast_to(1.0 / jnp.maximum(jnp.sum(count, axis=1, keepdims=True), 1.0), inv_ref.shape)
 
     def whiten(i, carry):
@@ -280,10 +297,8 @@
                     pl.ds((to * CHUNKS + q) * deep * PATCH_AZ, deep * PATCH_AZ), :
                 ].astype(jnp.bfloat16)
             got_rows[h, rank, q] = row_msg[h, rank, q]
-            if h == PHASES - 1:
-                for k in inner:
-                    to = partner(k) % near
-                    send(row_msg.at[h, to, q], got_rows.at[h, rank, q], row_send.at[0], row_recv.at[1 + q], partner(k))
+            if h == PHASES - 1 and q < AHEAD:
+                send_rows(q)
         if h < PHASES - 1:
             for k in inner:
                 to = partner(k) % near
@@ -301,8 +316,13 @@
             for o in range(n):
                 sum_msg[q, o, at, :] = out[o * PAIR : (o + 1) * PAIR]
         got_sums[q, me] = sum_msg[q, me]
-        for k in peers:
-            send(sum_msg.at[q, partner(k)], got_sums.at[q, me], sum_send.at[0], sum_recv.at[q], partner(k))
+        send_sums(q, range(near, n))
+
+        @pl.when(q + AHEAD < CHUNKS)
+        def _():
+            send_rows(q + AHEAD)
+
+        send_sums(q, inner)
         return carry
 
     lax.fori_loop(0, CHUNKS, reduce, 0)
@@ -353,8 +373,8 @@
             pltpu.VMEM(block, jnp.bfloat16),
             pltpu.VMEM(split, jnp.bfloat16),
             pltpu.VMEM(split, jnp.bfloat16),
-            pltpu.VMEM((FACTS, slots), jnp.float32),
-            pltpu.VMEM((n, FACTS, slots), jnp.float32),
+            pltpu.VMEM((2, slots // 2), jnp.float32),
+            pltpu.VMEM((n, 2, slots // 2), jnp.float32),
             pltpu.VMEM(block, jnp.float32),
             pltpu.VMEM((LANES // PATCH_RG, LANES, 2 * dates), jnp.bfloat16),
             pltpu.VMEM((PATCH_AZ, LANES, 2 * dates), jnp.bfloat16),

time: 65.2 us -> 61.8 us (0.948)
  Pallas kernels: 64 us -> 60.7 us
    pallas_call x1, Pallas kernels: 64 us -> 60.7 us  [shards(): pl.pallas_call(partial(flow_kernel, n), out_shape=jax.ShapeDtypeStruct((M...]
where the time goes in v5:
time: 61.8 us; the launch traced here: 61.7 us
  Pallas kernels  60.7 us (98%)
  local copies, waits for them, and re-layouts  0.97 us (2%)
    pallas_call x1, Pallas kernels, shards(): pl.pallas_call(partial(flow_kernel, n), out_shape=jax.ShapeDtypeStruct((M...  60.7 us

profile of v5, /device:TPU:0, one launch (start us, length us, event | category | flops | bytes accessed | tf_op | source)
XLA Modules:
  0.0 61.7 jit_solution(9173462328436388221)
XLA Ops:
  0.0 60.7 %flow.1 = f32[2048,128]{1,0:T(8,128)S(1)} custom-call(s32[8]{0:T(128)} %refs_0_.1, f32[4]{0:T(128)} %refs_1_.1, bf16[2,8,128,256]{3,2,1,0:T(8,128)(2,1)} %refs_2_.1, f32[2,8,128]{2,1,0:T(8,128)} %refs_3_.1, s32[1,16]{1,0:T(1,128)} %bitcast.6, s32[1,16]{1,0:T(1,128)} %bitcast.7, s32[1,16]{1,0:T(1,128)} %bitcast.8, s32[1,16]{1,0:T(1,128)} %bitcast.9), custom_call_target="tpu_custom_call" | custom-call | tf_op jit(solution)/shard_map/flow/pallas_call | solution.py:366
  60.7 1.0 %copy.10 = f32[8,256,128]{2,1,0:T(8,128)} copy(f32[8,256,128]{2,1,0:T(8,128)S(1)} %bitcast.5) | data formatting | bytes 2097152

commit v6 on v5

--- a/solution.py
+++ b/solution.py
@@ -17,8 +17,9 @@
 TOGETHER = 4
 SWEEPS = 3
 GROUPS = 2
-CHUNKS = 8
+CHUNKS = 4
 AHEAD = 2
+WIDE = 4
 FACTS = 8
 PAIR = 2 * PATCH_AZ
 
@@ -90,10 +91,11 @@
     inputs, refs = refs[:8], refs[8:]
     result_ref, cells_ref, got_cells, split_ref, got_split, facts_ref, got_facts, cell_ref, z_ref, white_ref, flat_ref = refs[:11]
     row_msg, got_rows, sum_msg, got_sums, operator_ref, spread_ref, shift_ref, inv_ref = refs[11:19]
-    work, local, refs = refs[19:23], refs[23:31], refs[31:]
+    wide_msg, got_wide, full_msg, got_full = refs[19:23]
+    work, local, refs = refs[23:27], refs[27:35], refs[35:]
     len_ref, kern_ref, radar_ref, taps_ref = local[:4]
     fact_refs = local[4:8]
-    own_sem, fact_send, fact_recv, cell_send, cell_recv, row_send, row_recv, sum_send, sum_recv, load_sem = refs
+    own_sem, fact_send, fact_recv, cell_send, cell_recv, row_send, row_recv, sum_send, sum_recv, wide_send, wide_recv, load_sem = refs
     me = lax.axis_index("date")
     dates_here, rows = radar_ref.shape[1], radar_ref.shape[2]
     taps, tile_count = taps_ref.shape[2], fact_refs[0].shape[1]
@@ -101,8 +103,9 @@
     windows = LANES // PATCH_RG
     near = n // GROUPS
     group, rank = me // near, me % near
-    slots = spread_ref.shape[1]
-    deep = 2 * total // near // CHUNKS
+    slots = spread_ref.shape[2]
+    deep = (2 * total - n * WIDE) // near // CHUNKS
+    start = n * WIDE
 
     barrier = pltpu.get_barrier_semaphore()
     loads = [pltpu.make_async_copy(x, y, load_sem.at[i]) for i, (x, y) in enumerate(zip(inputs, local))]
@@ -220,6 +223,10 @@
         for k in ks:
             send(sum_msg.at[q, partner(k)], got_sums.at[q, me], sum_send.at[0], sum_recv.at[q], partner(k))
 
+    def send_wide(h, ks):
+        for k in ks:
+            send(wide_msg.at[h, partner(k)], got_wide.at[h, me], wide_send.at[0], wide_recv.at[h], partner(k))
+
     def settle():
         drain(got_facts.at[pl.ds(0, n - 1)], fact_recv.at[0])
         from_at = lax.broadcasted_iota(jnp.int32, (tiles, slots), 0)
@@ -233,13 +240,14 @@
                 facts = facts + got_facts[k * near + s]
             return facts
 
-        here = jnp.concatenate([all_of(group), jnp.zeros((FACTS - 2, tiles), jnp.float32)], axis=0)
-        here = jnp.dot(here.astype(jnp.bfloat16), twice, preferred_element_type=jnp.float32)
-        row_at = lax.broadcasted_iota(jnp.int32, spread_ref.shape, 0)
-        slot_at = lax.broadcasted_iota(jnp.int32, spread_ref.shape, 1)
+        row_at = lax.broadcasted_iota(jnp.int32, spread_ref.shape[1:], 0)
+        slot_at = lax.broadcasted_iota(jnp.int32, spread_ref.shape[1:], 1)
         named = ((row_at >> 4) * MAP_DEV + (row_at & 7)).astype(jnp.float32)
-        same = jnp.logical_and(named == here[0:1], ((row_at ^ slot_at) & PATCH_AZ) == 0)
-        spread_ref[...] = jnp.where(same, here[1:2], 0.0).astype(jnp.bfloat16)
+        for k in range(GROUPS):
+            here = jnp.concatenate([all_of(k), jnp.zeros((FACTS - 2, tiles), jnp.float32)], axis=0)
+            here = jnp.dot(here.astype(jnp.bfloat16), twice, preferred_element_type=jnp.float32)
+            same = jnp.logical_and(named == here[0:1], ((row_at ^ slot_at) & PATCH_AZ) == 0)
+            spread_ref[k] = jnp.where(same, here[1:2], 0.0).astype(jnp.bfloat16)
         mine = (me * MAP_DEV + lax.broadcasted_iota(jnp.int32, (MAP_DEV, tiles), 0)).astype(jnp.float32)
         count = jnp.zeros((MAP_DEV, tiles), jnp.float32)
         for k in range(GROUPS):
@@ -272,6 +280,8 @@
             for u in range(2):
                 own[1 + u].wait()
                 drain(got_split.at[u, pl.ds(0, n - 1)], cell_recv.at[1 + u])
+                if u == 1:
+                    send_wide(0, range(n - 1, 0, -1))
                 for s in range(n):
                     cell_ref[s, : PATCH_AZ * dates_here] = got_split[u, s].astype(jnp.float32)
                 for part in range(2):
@@ -291,14 +301,19 @@
 
         for a in range(PATCH_AZ):
             flat_ref[pl.ds(a, 2 * total, stride=PATCH_AZ), :] = across(white_ref[a], shift_ref[a * 2 + h])
+        for o in range(n):
+            wide_msg[h, o] = flat_ref[pl.ds(o * WIDE * PATCH_AZ, WIDE * PATCH_AZ), :].astype(jnp.bfloat16)
+        got_wide[h, me] = wide_msg[h, me]
         for q in range(CHUNKS):
             for to in range(near):
                 row_msg[h, to, q] = flat_ref[
-                    pl.ds((to * CHUNKS + q) * deep * PATCH_AZ, deep * PATCH_AZ), :
+                    pl.ds((start + (to * CHUNKS + q) * deep) * PATCH_AZ, deep * PATCH_AZ), :
                 ].astype(jnp.bfloat16)
             got_rows[h, rank, q] = row_msg[h, rank, q]
             if h == PHASES - 1 and q < AHEAD:
                 send_rows(q)
+                if q == 0:
+                    send_wide(1, range(n - 1, 0, -1))
         if h < PHASES - 1:
             for k in inner:
                 to = partner(k) % near
@@ -312,7 +327,7 @@
         for i in range(deep // 2):
             at = slice(i * PAIR, (i + 1) * PAIR)
             cells = jnp.concatenate([got_rows[h, s, q, at, :] for h in range(PHASES) for s in range(near)], axis=0)
-            out = jnp.dot(spread_ref[...], cells, preferred_element_type=jnp.float32).astype(jnp.bfloat16)
+            out = jnp.dot(spread_ref[group], cells, preferred_element_type=jnp.float32).astype(jnp.bfloat16)
             for o in range(n):
                 sum_msg[q, o, at, :] = out[o * PAIR : (o + 1) * PAIR]
         got_sums[q, me] = sum_msg[q, me]
@@ -325,7 +340,26 @@
         send_sums(q, inner)
         return carry
 
-    lax.fori_loop(0, CHUNKS, reduce, 0)
+    def whole():
+        for h in range(PHASES):
+            drain(got_wide.at[h, pl.ds(0, n - 1)], wide_recv.at[h])
+        for i in range(WIDE // 2):
+            at = slice(i * PAIR, (i + 1) * PAIR)
+            out = jnp.zeros((n * PAIR, LANES), jnp.float32)
+            for k in range(GROUPS):
+                cells = jnp.concatenate(
+                    [got_wide[h, k * near + s, at, :] for h in range(PHASES) for s in range(near)], axis=0
+                )
+                out = out + jnp.dot(spread_ref[k], cells, preferred_element_type=jnp.float32)
+            for o in range(n):
+                full_msg[o, at, :] = out[o * PAIR : (o + 1) * PAIR].astype(jnp.bfloat16)
+        got_full[me] = full_msg[me]
+        for k in range(n - 1, 0, -1):
+            send(full_msg.at[partner(k)], got_full.at[me], wide_send.at[1], wide_recv.at[PHASES], partner(k))
+
+    lax.fori_loop(0, 2, reduce, 0)
+    whole()
+    lax.fori_loop(2, CHUNKS, reduce, 0)
 
     def finish(q, carry):
         drain(got_sums.at[q, pl.ds(0, n - 1)], sum_recv.at[q])
@@ -335,17 +369,26 @@
             for k in range(1, GROUPS):
                 y = y + got_sums[q, s + k * near].astype(jnp.float32)
             for r in range(deep):
-                at = pl.ds((s * CHUNKS + q) * deep + r, MAP_DEV, stride=2 * total)
+                at = pl.ds(start + (s * CHUNKS + q) * deep + r, MAP_DEV, stride=2 * total)
                 result_ref[at, :] = y[r * MAP_DEV : (r + 1) * MAP_DEV] * inv_ref[...]
         return carry
 
-    lax.fori_loop(0, CHUNKS, finish, 0)
+    lax.fori_loop(0, CHUNKS - 1, finish, 0)
+    drain(got_full.at[pl.ds(0, n - 1)], wide_recv.at[PHASES])
+    for s in range(n):
+        y = got_full[s].astype(jnp.float32)
+        for r in range(WIDE):
+            at = pl.ds(s * WIDE + r, MAP_DEV, stride=2 * total)
+            result_ref[at, :] = y[r * MAP_DEV : (r + 1) * MAP_DEV] * inv_ref[...]
+    finish(CHUNKS - 1, 0)
 
     drain(got_facts.at[pl.ds(0, n - 1)], fact_send.at[0])
     drain(cells_ref.at[pl.ds(0, n - 1)], cell_send.at[0])
     drain(split_ref.at[:, pl.ds(0, n - 1)], cell_send.at[1])
     drain(row_msg.at[:, pl.ds(0, near - 1)], row_send.at[0])
     drain(sum_msg.at[:, pl.ds(0, n - 1)], sum_send.at[0])
+    drain(wide_msg.at[:, pl.ds(0, n - 1)], wide_send.at[0])
+    drain(full_msg.at[pl.ds(0, n - 1)], wide_send.at[1])
 
 
 def shards(n, radar_stack, filter_taps, filter_lengths, resample_kernel, tile_owner, map_slot, correlation, offsets):
@@ -354,7 +397,7 @@
     tile_count = tile_owner.shape[0]
     near = n // GROUPS
     slots = PHASES * near * PAIR
-    deep = 2 * dates // near // CHUNKS
+    deep = (2 * dates - n * WIDE) // near // CHUNKS
     block = (n, 2 * PATCH_AZ * dates_here, LANES)
     split = (2, n, PATCH_AZ * dates_here, LANES)
     row_block = (PHASES, near, CHUNKS, deep * PATCH_AZ, LANES)
@@ -384,9 +427,13 @@
             pltpu.VMEM(sum_block, jnp.bfloat16),
             pltpu.VMEM(sum_block, jnp.bfloat16),
             pltpu.VMEM((dates_here, 2 * rows, 2 * rows), jnp.bfloat16),
-            pltpu.VMEM((n * PAIR, slots), jnp.bfloat16),
+            pltpu.VMEM((GROUPS, n * PAIR, slots), jnp.bfloat16),
             pltpu.VMEM((tile_count, TILE, TILE), jnp.bfloat16),
             pltpu.VMEM((MAP_DEV, LANES), jnp.float32),
+            pltpu.VMEM((PHASES, n, WIDE * PATCH_AZ, LANES), jnp.bfloat16),
+            pltpu.VMEM((PHASES, n, WIDE * PATCH_AZ, LANES), jnp.bfloat16),
+            pltpu.VMEM((n, WIDE * MAP_DEV, LANES), jnp.bfloat16),
+            pltpu.VMEM((n, WIDE * MAP_DEV, LANES), jnp.bfloat16),
             pltpu.VMEM((TOGETHER, dates, 2 * dates), jnp.float32),
             pltpu.VMEM((TOGETHER, LANES, 2 * dates), jnp.float32),
             pltpu.VMEM((TOGETHER, dates + LANES, 2 * dates), jnp.bfloat16),
@@ -408,6 +455,8 @@
             dma((1 + CHUNKS,)),
             dma((1,)),
             dma((CHUNKS,)),
+            dma((2,)),
+            dma((PHASES + 1,)),
             dma((len(given),)),
         ],
         compiler_params=pltpu.CompilerParams(collective_id=0, has_side_effects=True, vmem_limit_bytes=BIG),

time: 61.8 us -> 59.8 us (0.968)
  Pallas kernels: 60.7 us -> 58.6 us
    pallas_call x1, Pallas kernels: 60.7 us -> 58.6 us  [shards(): pl.pallas_call(partial(flow_kernel, n), out_shape=jax.ShapeDtypeStruct((M...]
where the time goes in v6:
time: 59.8 us; the launch traced here: 59.6 us
  Pallas kernels  58.6 us (98%)
  local copies, waits for them, and re-layouts  0.97 us (2%)
    pallas_call x1, Pallas kernels, shards(): pl.pallas_call(partial(flow_kernel, n), out_shape=jax.ShapeDtypeStruct((M...  58.6 us

profile of v6, /device:TPU:0, one launch (start us, length us, event | category | flops | bytes accessed | tf_op | source)
XLA Modules:
  0.0 59.6 jit_solution(16897294245075383607)
XLA Ops:
  0.0 58.6 %flow.1 = f32[2048,128]{1,0:T(8,128)S(1)} custom-call(s32[8]{0:T(128)} %refs_0_.1, f32[4]{0:T(128)} %refs_1_.1, bf16[2,8,128,256]{3,2,1,0:T(8,128)(2,1)} %refs_2_.1, f32[2,8,128]{2,1,0:T(8,128)} %refs_3_.1, s32[1,16]{1,0:T(1,128)} %bitcast.6, s32[1,16]{1,0:T(1,128)} %bitcast.7, s32[1,16]{1,0:T(1,128)} %bitcast.8, s32[1,16]{1,0:T(1,128)} %bitcast.9), custom_call_target="tpu_custom_call" | custom-call | tf_op jit(solution)/shard_map/flow/pallas_call | solution.py:409
  58.6 1.0 %copy.10 = f32[8,256,128]{2,1,0:T(8,128)} copy(f32[8,256,128]{2,1,0:T(8,128)S(1)} %bitcast.5) | data formatting | bytes 2097152

commit v7 on v6

--- a/solution.py
+++ b/solution.py
@@ -18,7 +18,7 @@
 SWEEPS = 3
 GROUPS = 2
 CHUNKS = 4
-AHEAD = 2
+AHEAD = 3
 WIDE = 4
 FACTS = 8
 PAIR = 2 * PATCH_AZ
@@ -95,7 +95,7 @@
     work, local, refs = refs[23:27], refs[27:35], refs[35:]
     len_ref, kern_ref, radar_ref, taps_ref = local[:4]
     fact_refs = local[4:8]
-    own_sem, fact_send, fact_recv, cell_send, cell_recv, row_send, row_recv, sum_send, sum_recv, wide_send, wide_recv, load_sem = refs
+    own_sem, fact_send, fact_recv, cell_send, cell_recv, row_send, row_recv, sum_send, sum_recv, wide_send, wide_recv, load_sem, ready_sem = refs
     me = lax.axis_index("date")
     dates_here, rows = radar_ref.shape[1], radar_ref.shape[2]
     taps, tile_count = taps_ref.shape[2], fact_refs[0].shape[1]
@@ -111,8 +111,6 @@
     loads = [pltpu.make_async_copy(x, y, load_sem.at[i]) for i, (x, y) in enumerate(zip(inputs, local))]
     for load in loads:
         load.start()
-    for k in range(1, n):
-        pl.semaphore_signal(barrier, inc=1, device_id={"date": lax.rem(me + k, n)}, device_id_type=MESH)
     own = [pltpu.make_async_copy(cells_ref.at[me], got_cells.at[me], own_sem.at[0])]
     own += [pltpu.make_async_copy(split_ref.at[u, me], got_split.at[u, me], own_sem.at[1 + u]) for u in range(2)]
 
@@ -138,6 +136,23 @@
 
     def turn(i):
         return n - 1 - i // 2 - i % 2 * (n // 2)
+
+    quarter = n // 4
+    middle = (me // quarter) % 2 != me // (2 * quarter)
+    close = list(range(1, 2 * quarter))
+    beside = list(range(3 * quarter, n))
+    apart = list(range(2 * quarter, 3 * quarter))
+
+    def tell(sem, k):
+        pl.semaphore_signal(sem, inc=1, device_id={"date": partner(k)}, device_id_type=MESH)
+
+    for k in close:
+        tell(barrier, k)
+
+    @pl.when(middle)
+    def _():
+        for k in beside:
+            tell(barrier, k)
 
     peers = [turn(i) for i in range(n - 1)]
     inner = list(range(near - 1, 0, -1))
@@ -184,12 +199,30 @@
         if h == 0:
             for p in range(n):
                 cells_ref[p] = cell_ref[p].astype(jnp.bfloat16)
-            pl.semaphore_wait(barrier, n - 1)
-            for k in peers:
-                send(facts_ref, got_facts.at[me], fact_send.at[0], fact_recv.at[0], partner(k))
+
+            def first(ks):
+                for k in ks:
+                    send(facts_ref, got_facts.at[me], fact_send.at[0], fact_recv.at[0], partner(k))
+                    send(cells_ref.at[partner(k)], got_cells.at[me], cell_send.at[0], cell_recv.at[0], partner(k))
+
             got_facts[me] = facts_ref[...]
-            for k in peers:
-                send(cells_ref.at[partner(k)], got_cells.at[me], cell_send.at[0], cell_recv.at[0], partner(k))
+
+            @pl.when(middle)
+            def _():
+                pl.semaphore_wait(barrier, len(close) + len(beside))
+                tell(ready_sem, 3 * quarter)
+                first(beside)
+                pl.semaphore_wait(ready_sem, 1)
+                tell(ready_sem, quarter)
+                first([k for pair in zip(apart, close[quarter - 1 :][::-1]) for k in pair])
+                first(close[: quarter - 1])
+
+            @pl.when(jnp.logical_not(middle))
+            def _():
+                pl.semaphore_wait(barrier, len(close))
+                pl.semaphore_wait(ready_sem, 1)
+                first(peers)
+
             own[0].start()
         else:
             low = lax.broadcasted_iota(jnp.int32, (PATCH_AZ * dates_here, LANES), 1) < LANES // 2
@@ -205,10 +238,10 @@
                     )
                 own[1 + u].start()
 
-    apart = lax.broadcasted_iota(jnp.int32, (TILE, TILE), 0) - lax.broadcasted_iota(jnp.int32, (TILE, TILE), 1) + TILE
+    turned = lax.broadcasted_iota(jnp.int32, (TILE, TILE), 0) - lax.broadcasted_iota(jnp.int32, (TILE, TILE), 1) + TILE
     for t in range(tile_count):
         shift = fact_refs[2][:, t : t + 1]
-        step = (apart - shift) & (TILE - 1)
+        step = (turned - shift) & (TILE - 1)
         circ = jnp.zeros((TILE, TILE), jnp.float32)
         for k in range(KW):
             circ = jnp.where(step == k, kern_ref[k], circ)
@@ -458,6 +491,7 @@
             dma((2,)),
             dma((PHASES + 1,)),
             dma((len(given),)),
+            pltpu.SemaphoreType.REGULAR,
         ],
         compiler_params=pltpu.CompilerParams(collective_id=0, has_side_effects=True, vmem_limit_bytes=BIG),
         name="flow",

time: 59.8 us -> 58.4 us (0.977)
  Pallas kernels: 58.6 us -> 57.2 us
    pallas_call x1, Pallas kernels: 58.6 us -> 57.2 us  [shards(): pl.pallas_call(partial(flow_kernel, n), out_shape=jax.ShapeDtypeStruct((M...]
where the time goes in v7:
time: 58.4 us; the launch traced here: 58.2 us
  Pallas kernels  57.2 us (98%)
  local copies, waits for them, and re-layouts  0.97 us (2%)
    pallas_call x1, Pallas kernels, shards(): pl.pallas_call(partial(flow_kernel, n), out_shape=jax.ShapeDtypeStruct((M...  57.2 us

profile of v7, /device:TPU:0, one launch (start us, length us, event | category | flops | bytes accessed | tf_op | source)
XLA Modules:
  0.0 58.2 jit_solution(11662684620404254746)
XLA Ops:
  0.0 57.2 %flow.1 = f32[2048,128]{1,0:T(8,128)S(1)} custom-call(s32[8]{0:T(128)} %refs_0_.1, f32[4]{0:T(128)} %refs_1_.1, bf16[2,8,128,256]{3,2,1,0:T(8,128)(2,1)} %refs_2_.1, f32[2,8,128]{2,1,0:T(8,128)} %refs_3_.1, s32[1,16]{1,0:T(1,128)} %bitcast.6, s32[1,16]{1,0:T(1,128)} %bitcast.7, s32[1,16]{1,0:T(1,128)} %bitcast.8, s32[1,16]{1,0:T(1,128)} %bitcast.9), custom_call_target="tpu_custom_call" | custom-call | tf_op jit(solution)/shard_map/flow/pallas_call | solution.py:442
  57.2 1.0 %copy.10 = f32[8,256,128]{2,1,0:T(8,128)} copy(f32[8,256,128]{2,1,0:T(8,128)S(1)} %bitcast.5) | data formatting | bytes 2097152
